TPU v7x, 128 devices: a whole 4x4x4 slice. The times are simulated.
128 devices in a mesh: dp: 64 (over x, z, y), mp: 2 (over core).
Axes of the slice: x: 4, y: 4, z: 4, core: 2. Of those that a mesh axis runs over, the one named last changes fastest.
Arguments:
- features: bfloat16 [32768, 2048], P('dp', 'mp'), may hold values from -6 to 6
- gains: float32 [2, 2048], replicated, may hold values from 0.25 to 1.75
- weights: bfloat16 [2, 2048, 2048], P(None, None, 'mp'), may hold values from -0.125 to 0.125
- heads: bfloat16 [4096, 32, 2048], P('dp', None, 'mp'), may hold values from -0.125 to 0.125
- lengths: int32 [64, 64], P('dp'), may hold values from 1 to 8, 256 in all within a row
- owners: int32 [64, 64], P('dp'), may hold values from 0 to 63, each once within a row
- labels: int32 [32768], P('dp'), may hold values from 0 to 31
Outputs:
- body_grads: float32 [2, 2048, 2048], P(None, 'dp', 'mp')
- token_loss: bfloat16 [32768], P('dp')
Inputs may be any that keep to these rules, and one draw needn't show every extreme that they name: `lengths`: each row (one block's 64 clients) holds token counts of 1 to 8 that sum to 256; some client of each block holds exactly 8. `owners`: each row names every head owner 0 to 63 exactly once.
All inputs are finite; a program needn't handle non-finite values.
Results may differ from a plain program's by a relative error of at most 0.0073.
Values may be sent and summed in bfloat16 or wider, within the bound.
A program may use at most 128 MiB of HBM per device.

v0:
```python
import functools

import jax
import jax.numpy as jnp
from jax import lax
from jax.experimental import pallas as pl
from jax.experimental.pallas import tpu as pltpu
from jax.sharding import PartitionSpec as P

EPSILON = 1e-06
MESH = pl.DeviceIdType.MESH
STRIDES = (16, 4, 1)
WIDTHS = ((384, 256, 384), (384, 384, 256))
STARTS = tuple(tuple(sum(w[:k]) for k in range(3)) for w in WIDTHS)
UNITS = (32, 8, 2)

def blend(core, a, b):
    return a + core * (b - a)

class Ring:
    def __init__(self, me, core, bufs):
        self.me, self.core = me, core
        self.g, self.t1, self.t2, self.rx, self.tx, self.ssem, self.rsem = bufs
        self.coords = tuple((me // s) % 4 for s in STRIDES)

    def dim(self, c, ph):
        k0, k1 = (c + ph) % 3, (c + ph + 1) % 3
        stride = blend(self.core, STRIDES[k0], STRIDES[k1])
        p = blend(self.core, self.coords[k0], self.coords[k1])
        right = self.me + ((p + 1) % 4 - p) * stride
        left = self.me + ((p + 3) % 4 - p) * stride
        return p, right, left

    def src(self, l, c, ph):
        return (self.g, self.t1, self.t2)[ph][l * 3 + c]

    def copy(self, l, c, ph, k, src, to):
        n = l * 3 + c
        return pltpu.make_async_remote_copy(
            src_ref=src, dst_ref=self.rx[ph][n].at[k],
            send_sem=self.ssem.at[n, ph, k], recv_sem=self.rsem.at[n, ph, k],
            device_id=(to, self.core), device_id_type=MESH)

    def copies(self, l, c, ph):
        p, right, left = self.dim(c, ph)
        P, H, tx = self.src(l, c, ph), UNITS[ph] // 2, self.tx[ph][l * 3 + c]
        half = (pl.ds(0, H), pl.ds(H, H))
        def nth(k):
            if k < 4:
                src = P.at[(p + (2, 1, 2, 3)[k]) % 4, half[(0, 1, 1, 0)[k]]]
            else:
                src = tx.at[k - 4]
            return self.copy(l, c, ph, k, src, (right, right, left, left, right, left)[k])
        return nth

    def start_a(self, l, c, ph):
        cp = self.copies(l, c, ph)
        for k in (0, 2, 1, 3):
            cp(k).start()

    def step_b(self, l, c, ph):
        cp = self.copies(l, c, ph)
        p, _, _ = self.dim(c, ph)
        P, H = self.src(l, c, ph), UNITS[ph] // 2
        rx, tx = self.rx[ph][l * 3 + c], self.tx[ph][l * 3 + c]
        for k, q, off in ((0, (p + 1) % 4, 0), (2, (p + 3) % 4, H)):
            cp(k).wait_recv()
            def add(u, n):
                tx[k // 2, pl.ds(u, n)] = (P[q, pl.ds(off + u, n)].astype(jnp.float32) + rx[k, pl.ds(u, n)].astype(jnp.float32)).astype(jnp.bfloat16)
            self.each(H, add)
            cp(4 + k // 2).start()

    def finish(self, l, c, ph, store):
        cp = self.copies(l, c, ph)
        p, _, _ = self.dim(c, ph)
        P, H = self.src(l, c, ph), UNITS[ph] // 2
        rx = self.rx[ph][l * 3 + c]
        for a, b, off in ((3, 4, 0), (1, 5, H)):
            cp(a).wait_recv()
            cp(b).wait_recv()
            def add(u, n):
                store(off + u, n, P[p, pl.ds(off + u, n)].astype(jnp.float32) + rx[a, pl.ds(u, n)].astype(jnp.float32) + rx[b, pl.ds(u, n)].astype(jnp.float32))
            self.each(H, add)

    @staticmethod
    def each(count, f):
        n = min(count, 4)
        if count == n:
            f(0, n)
        else:
            def body(i, c):
                f(pl.multiple_of(i * n, n), n)
                return c
            lax.fori_loop(0, count // n, body, 0)

    def next_phase(self, l, c, ph):
        t = (self.t1, self.t2)[ph][l * 3 + c]
        per = UNITS[ph + 1]
        def store(u, n, v):
            m = min(n, per)
            for j in range(0, n, m):
                q, r = (u + j) // per, (u + j) % per
                t[q, pl.ds(r, m)] = v[j:j + m].astype(jnp.bfloat16)
        self.finish(l, c, ph, store)
        self.start_a(l, c, ph + 1)

    def last(self, l, c, out):
        w0, w = STARTS[l][c], WIDTHS[l][c]
        def store(u, n, v):
            for j in range(n):
                out[l, (u + j) * 16:(u + j + 1) * 16, w0:w0 + w] = v[j]
        self.finish(l, c, 2, store)

    def put_partial(self, l, x, z, y, val):
        xyz = (x, z, y)
        v = val.astype(jnp.bfloat16).reshape(2, 16, 1024)
        for c in range(3):
            a, b, d = (blend(self.core, xyz[(c + k) % 3], xyz[(c + k + 1) % 3]) for k in range(3))
            w0, w = STARTS[l][c], WIDTHS[l][c]
            self.g[l * 3 + c][a, pl.ds((b * 4 + d) * 2, 2)] = v[:, :, w0:w0 + w]

    def wait_sends(self):
        for l in range(2):
            for c in range(3):
                for ph in range(3):
                    for k in range(6):
                        self.copies(l, c, ph)(k).wait_send()

def scratch():
    lc = [(l, c) for l in range(2) for c in range(3)]
    bf = jnp.bfloat16
    return [
        [pltpu.VMEM((4, 32, 16, WIDTHS[l][c]), bf) for l, c in lc],
        [pltpu.VMEM((4, 8, 16, WIDTHS[l][c]), bf) for l, c in lc],
        [pltpu.VMEM((4, 2, 16, WIDTHS[l][c]), bf) for l, c in lc],
        [[pltpu.VMEM((6, n // 2, 16, WIDTHS[l][c]), bf) for l, c in lc] for n in UNITS],
        [[pltpu.VMEM((2, n // 2, 16, WIDTHS[l][c]), bf) for l, c in lc] for n in UNITS],
        pltpu.SemaphoreType.DMA((6, 3, 6)),
        pltpu.SemaphoreType.DMA((6, 3, 6)),
    ]

def flat(tree):
    return jax.tree.flatten(tree, is_leaf=lambda v: not isinstance(v, list))

def enter(me, core):
    bar = pltpu.get_barrier_semaphore()
    for s in STRIDES:
        p = (me // s) % 4
        for step in (1, 3):
            pl.semaphore_signal(bar, inc=1, device_id=(me + ((p + step) % 4 - p) * s, core), device_id_type=MESH)
    pl.semaphore_wait(bar, 6)

def partials(ring, l, nt_ref, delta_ref):
    def group(x, carry):
        rows = pl.ds(pl.multiple_of(x * 512, 512), 512)
        prod = jnp.dot(nt_ref[l, rows, :], delta_ref[l], preferred_element_type=jnp.float32)
        for z in range(4):
            for y in range(4):
                b = (z * 4 + y) * 32
                ring.put_partial(l, x, z, y, prod[b:b + 32])
        return carry
    lax.fori_loop(0, 4, group, 0)

def rs_kernel(tree, nt_ref, delta_ref, out, *refs):
    me, core = lax.axis_index("dp"), lax.axis_index("mp")
    ring = Ring(me, core, jax.tree.unflatten(tree, refs))
    enter(me, core)
    order = (1, 0)
    for l in order:
        partials(ring, l, nt_ref, delta_ref)
        for c in range(3):
            ring.start_a(l, c, 0)
    for ph in range(3):
        for l in order:
            for c in range(3):
                ring.step_b(l, c, ph)
        for l in order:
            for c in range(3):
                if ph < 2:
                    ring.next_phase(l, c, ph)
                else:
                    ring.last(l, c, out)
    ring.wait_sends()

def rs_call(nt, delta, cid=0):
    leaves, tree = flat(scratch())
    return pl.pallas_call(functools.partial(rs_kernel, tree),
        out_shape=jax.ShapeDtypeStruct((2, 32, 1024), jnp.float32),
        in_specs=[pl.BlockSpec(memory_space=pltpu.VMEM)] * 2,
        out_specs=pl.BlockSpec(memory_space=pltpu.VMEM),
        scratch_shapes=leaves,
        compiler_params=pltpu.CompilerParams(collective_id=cid, has_side_effects=True, vmem_limit_bytes=56 << 20),
        name="grad_rs")(nt, delta)


def sent_to_all(value, axis):
    devices = lax.axis_size(axis)
    return lax.all_to_all(
        jnp.broadcast_to(value[None], (devices, *value.shape)), axis, 0, 0, tiled=True
    )


def widen_rows(narrow):
    tiles = jnp.moveaxis(sent_to_all(narrow, "mp"), 0, 1)
    return tiles.reshape(narrow.shape[0], -1)


def of_everyone(value, axis):
    return sent_to_all(value, axis).sum(axis=0)


def sum_at_owner(value, axis):
    rows, cols = value.shape
    devices = lax.axis_size(axis)
    tiles = jnp.moveaxis(value.reshape(rows, devices, cols // devices), 1, 0)
    arrived = lax.all_to_all(tiles, axis, split_axis=0, concat_axis=0, tiled=True)
    return arrived.astype(jnp.float32).sum(axis=0)


def gelu_back(pre_act, upstream):
    return jax.vjp(jax.nn.gelu, pre_act)[1](upstream)[0]


def norm_layer(full_rows, own_cols, norm_gain, weight):
    widened = full_rows.astype(jnp.float32)
    rms_scale = lax.rsqrt(jnp.mean(widened * widened, -1, keepdims=True) + EPSILON)
    normed = (widened * rms_scale * norm_gain).astype(jnp.bfloat16)
    pre_act = jnp.dot(normed, weight, preferred_element_type=jnp.float32)
    outputs = (own_cols.astype(jnp.float32) + jax.nn.gelu(pre_act)).astype(jnp.bfloat16)
    return (normed, rms_scale, pre_act, outputs)


def body(features, gains, weights, heads, lengths, owners, labels):
    slots, half_width = features.shape
    groups = lax.axis_size("dp")
    classes = heads.shape[1]
    live = slots // 2
    block_heads = lax.all_to_all(heads, "dp", 0, 0, tiled=True)
    own_first = features[:live]
    rows_first = widen_rows(own_first)
    full_width = rows_first.shape[1]
    normed_first, scale_first, pre_first, hidden_mid = norm_layer(
        rows_first, own_first, gains[0], weights[0]
    )
    rows_second = widen_rows(hidden_mid)
    normed_second, scale_second, pre_second, hidden_top = norm_layer(
        rows_second, hidden_mid, gains[1], weights[1]
    )
    ends = jnp.cumsum(lengths[0])
    slot = lax.broadcasted_iota(jnp.int32, (groups, live), 1)
    here = (slot < ends[:, None]) & (slot >= (ends - lengths[0])[:, None])
    slot_owner = jnp.sum(jnp.where(here, owners[0][:, None], 0), 0)
    slot_len = jnp.sum(jnp.where(here, lengths[0][:, None], 0), 0)
    mine = lax.broadcasted_iota(jnp.int32, (groups, live), 0) == slot_owner[None, :]
    all_logits = lax.dot_general(
        block_heads, hidden_top, (((2,), (1,)), ((), ())), preferred_element_type=jnp.float32
    )
    part = jnp.sum(jnp.where(mine[:, None, :], all_logits, 0.0), 0)
    logits = of_everyone(part, "mp")
    hit = lax.broadcasted_iota(jnp.int32, (classes, live), 0) == labels[:live][None, :]
    log_total = jnp.log(jnp.sum(jnp.exp(logits), 0))
    losses = (log_total - jnp.sum(jnp.where(hit, logits, 0.0), 0)).astype(jnp.bfloat16)
    dlogits = (
        (jnp.exp(logits - log_total[None]) - hit.astype(jnp.float32))
        * (1.0 / slot_len.astype(jnp.float32))[None]
    ).astype(jnp.bfloat16)
    spread = jnp.where(mine[:, None, :], dlogits[None], jnp.zeros((), jnp.bfloat16))
    upstream = (
        lax.dot_general(
            spread, block_heads, (((0, 1), (0, 1)), ((), ())), preferred_element_type=jnp.float32
        )
        .astype(jnp.bfloat16)
        .astype(jnp.float32)
    )
    delta_second = gelu_back(pre_second, upstream).astype(jnp.bfloat16)
    dnormed_part = lax.dot_general(
        delta_second, weights[1], (((1,), (1,)), ((), ())), preferred_element_type=jnp.float32
    )
    gain_cols = lax.dynamic_slice_in_dim(gains[1], lax.axis_index("mp") * half_width, half_width, 0)
    hidden_cols = hidden_mid.astype(jnp.float32)
    dnormed = sum_at_owner(dnormed_part.astype(jnp.bfloat16), "mp")
    cross_term = of_everyone(jnp.sum(hidden_cols * gain_cols * dnormed, -1), "mp") / full_width
    dhidden = (
        upstream
        + gain_cols * scale_second * dnormed
        - hidden_cols * scale_second**3 * cross_term[:, None]
    )
    delta_first = gelu_back(pre_first, dhidden).astype(jnp.bfloat16)
    grads = rs_call(
        jnp.stack([normed_first.T, normed_second.T]), jnp.stack([delta_first, delta_second])
    )
    return (grads, jnp.concatenate([losses, jnp.zeros((slots - live,), jnp.bfloat16)]))


def solution(mesh):
    return jax.shard_map(
        body,
        mesh=mesh,
        in_specs=(
            P("dp", "mp"),
            P(),
            P(None, None, "mp"),
            P("dp", None, "mp"),
            P("dp", None),
            P("dp", None),
            P("dp"),
        ),
        out_specs=(P(None, "dp", "mp"), P("dp")),
        check_vma=False,
    )
```

profile of v0, /device:TPU:0, one launch (start us, length us, event | category | flops | bytes accessed | tf_op | source)
XLA Modules:
  0.0 181.9 jit_solution(14498449297811889878)
XLA Ops:
  0.6 1.1 slice.20
  1.7 0.2 copy.29
  1.9 1.1 broadcast_in_dim.62
  3.0 3.6 %all-to-all-start = ((bf16[2,256,1024]{1,2,0:T(8,128)(2,1)}), bf16[2,256,1024]{1,2,0:T(8,128)(2,1)S(1)}, u32[]{:S(2)}, u32[]{:S(2)}) async-start(bf16[2,256,1024]{1,2,0:T(8,128)(2,1)} %broadcast_in_dim.62), calls=%async_computation | async-start | bytes 2097152 | tf_op jit(solution)/shard_map/all_to_all | solution.py:198
  6.7 2.0 %all-to-all-done = bf16[2,256,1024]{1,2,0:T(8,128)(2,1)S(1)} async-done(((bf16[2,256,1024]{1,2,0:T(8,128)(2,1)}), bf16[2,256,1024]{1,2,0:T(8,128)(2,1)S(1)}, u32[]{:S(2)}, u32[]{:S(2)}) %all-to-all-start) | async-done | bytes 1048608 | tf_op jit(solution)/shard_map/all_to_all | solution.py:198
  8.7 0.3 multiply_reduce_fusion.1
  9.0 0.3 multiply_convert_fusion.1
  9.4 4.7 %add_convert_fusion = (bf16[256,1024]{1,0:T(8,128)(2,1)S(1)}, f32[256,1024]{1,0:T(8,128)}) fusion(bf16[512,1024]{1,0:T(8,128)(2,1)S(1)} %copy-done.1, bf16[256,2048]{0,1:T(8,128)(2,1)S(1)} %bitcast.75, bf16[2,2048,1024]{2,1,0:T(8,128)(2,1)} %param.9), kind=kOutput, calls=%fused_computation.65 | convolution fusion | flops 1076625408 | bytes 7340032 | tf_op jit(solution)/shard_map/dot_general | solution.py:228
  14.0 0.2 copy.30
  14.3 4.6 %all_to_all.31 = bf16[2,256,1024]{1,2,0:T(8,128)(2,1)S(1)} all-to-all(bf16[2,256,1024]{1,2,0:T(8,128)(2,1)S(1)} %broadcast_in_dim.94), channel_id=1, replica_groups=mesh['dp'=64,'mp'=2] {'mp'}, dimensions={0} | all-to-all | bytes 2097152 | tf_op jit(solution)/shard_map/all_to_all | solution.py:198
  18.9 11.9 %all-to-all-start.2 = ((bf16[64,32,1024]{2,1,0:T(8,128)(2,1)}), bf16[64,32,1024]{2,1,0:T(8,128)(2,1)}, u32[]{:S(2)}, u32[]{:S(2)}) async-start(bf16[64,32,1024]{2,1,0:T(8,128)(2,1)} %param.10), calls=%async_computation.2 | async-start | bytes 8388608 | tf_op jit(solution)/shard_map/all_to_all | solution.py:238
  31.2 0.1 select_reduce_fusion
  31.3 0.3 multiply_reduce_fusion
  31.7 0.3 fusion.19
  32.0 0.3 fusion.17
  32.4 1.5 pad_maximum_fusion.nt_ref
  33.9 0.3 multiply_convert_fusion
  34.2 4.5 %fusion.2 = f32[256,1024]{1,0:T(8,128)} fusion(bf16[256,2048]{0,1:T(8,128)(2,1)S(1)} %bitcast.76, bf16[2,2048,1024]{2,1,0:T(8,128)(2,1)} %param.9), kind=kOutput, calls=%fused_computation.2 | convolution fusion | flops 1073741824 | bytes 6291456 | tf_op jit(solution)/shard_map/dot_general | solution.py:228
  38.7 47.0 %all-to-all-done.2 = bf16[64,32,1024]{2,1,0:T(8,128)(2,1)} async-done(((bf16[64,32,1024]{2,1,0:T(8,128)(2,1)}), bf16[64,32,1024]{2,1,0:T(8,128)(2,1)}, u32[]{:S(2)}, u32[]{:S(2)}) %all-to-all-start.2) | async-done | bytes 4194336 | tf_op jit(solution)/shard_map/all_to_all | solution.py:238
  85.6 7.5 %fusion.20 = f32[32,256]{1,0:T(8,128)S(1)} fusion(bf16[64,32,1024]{2,1,0:T(8,128)(2,1)} %all-to-all-done.2, pred[64,256]{1,0:T(8,128)(4,1)S(1)} %iota_compare_fusion.2, bf16[256,1024]{1,0:T(8,128)(2,1)S(1)} %get-tuple-element.14, f32[256,1024]{1,0:T(8,128)} %fusion.2), kind=kOutput, calls=%fused_computation.22 | convolution fusion | flops 1077665792 | bytes 5816320 | tf_op jit(solution)/shard_map/dot_general | solution.py:255
  93.2 3.8 %all_to_all.32 = f32[2,32,256]{2,1,0:T(8,128)S(1)} all-to-all(f32[2,32,256]{2,1,0:T(8,128)S(1)} %broadcast_in_dim.100), channel_id=1, replica_groups=mesh['dp'=64,'mp'=2] {'mp'}, dimensions={0} | all-to-all | bytes 131072 | tf_op jit(solution)/shard_map/all_to_all | solution.py:198
  97.1 8.4 %fusion.42 = (bf16[256,1024]{1,0:T(8,128)(2,1)S(1)}, bf16[256,1024]{1,0:T(8,128)(2,1)}) fusion(f32[256,1024]{1,0:T(8,128)S(1)} %copy-done.6, bf16[64,32,1024]{2,1,0:T(8,128)(2,1)} %all-to-all-done.2, pred[64,256]{1,0:T(8,128)(4,1)S(1)} %iota_compare_fusion.2, bf16[32,256]{1,0:T(8,128)(2,1)S(1)} %multiply_convert_fusion.2), kind=kOutput, calls=%fused_computation.53 | convolution fusion | flops 1080033280 | bytes 6324224 | tf_op jit(solution)/shard_map/dot_general | solution.py:269
  105.5 3.5 %fusion.13 = bf16[256,2048]{1,0:T(8,128)(2,1)S(1)} fusion(bf16[256,1024]{1,0:T(8,128)(2,1)S(1)} %get-tuple-element.16, bf16[2,2048,1024]{2,1,0:T(8,128)(2,1)} %param.9), kind=kOutput, calls=%fused_computation.13 | convolution fusion | flops 1074266112 | bytes 5767168 | tf_op jit(solution)/shard_map/dot_general | solution.py:276
  109.1 4.6 %all_to_all.33 = bf16[2,256,1024]{2,1,0:T(8,128)(2,1)S(1)} all-to-all(bf16[2,256,1024]{2,1,0:T(8,128)(2,1)S(1)} %bitcast.71), channel_id=1, replica_groups=mesh['dp'=64,'mp'=2] {'mp'}, dimensions={0} | all-to-all | bytes 2097152 | tf_op jit(solution)/shard_map/all_to_all | solution.py:216
  113.7 0.2 convert_reduce_fusion
  113.9 0.2 fusion.47
  114.1 3.7 %all_to_all.34 = f32[2,1,256]{2,1,0:T(1,128)S(1)} all-to-all(f32[2,1,256]{2,1,0:T(1,128)S(1)} %broadcast_in_dim.104), channel_id=1, replica_groups=mesh['dp'=64,'mp'=2] {'mp'}, dimensions={0} | all-to-all | bytes 4096 | tf_op jit(solution)/shard_map/all_to_all | solution.py:198
  117.8 2.1 %fusion.60 = bf16[1,256,1024]{2,1,0:T(8,128)(2,1)S(1)} fusion(f32[256,1024]{1,0:T(8,128)S(1)} %copy-done, f32[256]{0:T(256)S(1)} %broadcast_multiply_fusion, f32[256]{0:T(256)S(1)} %get-tuple-element.12, bf16[256,1024]{1,0:T(8,128)(2,1)S(1)} %get-tuple-element.14, f32[256,1024]{1,0:T(8,128)S(1)} %convert_reduce_fusion, f32[256]{0:T(256)S(1)} %get-tuple-element.13, ...), kind=kLoop, calls=%fused_computation.73 | loop fusion | flops 7340032 | bytes 3677184 | tf_op jit(solution)/shard_map/stack | solution.py:290
  119.9 1.1 pad_maximum_fusion.1.delta_ref
  121.0 58.6 %grad_rs.1 = f32[2,32,1024]{2,1,0:T(8,128)} custom-call(bf16[2,2048,256]{2,1,0:T(8,128)(2,1)} %pad_maximum_fusion.nt_ref, bf16[2,256,1024]{2,1,0:T(8,128)(2,1)} %pad_maximum_fusion.1.delta_ref), custom_call_target="tpu_custom_call" | custom-call | tf_op jit(solution)/shard_map/grad_rs/pallas_call | solution.py:187
  179.7 0.6 concatenate.3
  180.2 1.7 copy.53
  (37 shorter events, 0.7 us)
Async XLA Ops:
  1.9 4.7 %copy-start.2 = (f32[2,2048]{1,0:T(2,128)S(1)}, f32[2,2048]{1,0:T(2,128)}, u32[]{:S(2)}) copy-start(f32[2,2048]{1,0:T(2,128)} %param.8) | copy-start | bytes 49156
  3.0 5.7 %all-to-all-start = ((bf16[2,256,1024]{1,2,0:T(8,128)(2,1)}), bf16[2,256,1024]{1,2,0:T(8,128)(2,1)S(1)}, u32[]{:S(2)}, u32[]{:S(2)}) async-start(bf16[2,256,1024]{1,2,0:T(8,128)(2,1)} %broadcast_in_dim.62), calls=%async_computation | async-start | bytes 2097152 | tf_op jit(solution)/shard_map/all_to_all | solution.py:198
  6.6 2.8 %copy-start.1 = (bf16[512,1024]{1,0:T(8,128)(2,1)S(1)}, bf16[512,1024]{1,0:T(8,128)(2,1)}, u32[]{:S(2)}) copy-start(bf16[512,1024]{1,0:T(8,128)(2,1)} %param.7) | copy-start | bytes 3145732
  18.9 12.0 %copy-start.3 = (s32[1,64]{1,0:T(1,128)S(1)}, s32[1,64]{1,0:T(1,128)}, u32[]{:S(2)}) copy-start(s32[1,64]{1,0:T(1,128)} %param.11) | copy-start | bytes 772
  18.9 12.3 %copy-start.4 = (s32[512]{0:T(512)S(1)}, s32[512]{0:T(512)}, u32[]{:S(2)}) copy-start(s32[512]{0:T(512)} %param.13) | copy-start | bytes 6148
  18.9 12.3 %copy-start.5 = (s32[1,64]{1,0:T(1,128)S(1)}, s32[1,64]{1,0:T(1,128)}, u32[]{:S(2)}) copy-start(s32[1,64]{1,0:T(1,128)} %param.12) | copy-start | bytes 772
  18.9 66.8 %all-to-all-start.2 = ((bf16[64,32,1024]{2,1,0:T(8,128)(2,1)}), bf16[64,32,1024]{2,1,0:T(8,128)(2,1)}, u32[]{:S(2)}, u32[]{:S(2)}) async-start(bf16[64,32,1024]{2,1,0:T(8,128)(2,1)} %param.10), calls=%async_computation.2 | async-start | bytes 8388608 | tf_op jit(solution)/shard_map/all_to_all | solution.py:238
  38.7 58.4 %copy-start.6 = (f32[256,1024]{1,0:T(8,128)S(1)}, f32[256,1024]{1,0:T(8,128)}, u32[]{:S(2)}) copy-start(f32[256,1024]{1,0:T(8,128)} %fusion.2) | copy-start | bytes 3145732
  113.7 4.2 %copy-start = (f32[256,1024]{1,0:T(8,128)S(1)}, f32[256,1024]{1,0:T(8,128)}, u32[]{:S(2)}) copy-start(f32[256,1024]{1,0:T(8,128)} %get-tuple-element.15) | copy-start | bytes 3145732
where the time goes:
time: 183 us; the launch traced here: 182 us
  Pallas kernels  58.6 us (32%)
  waiting for transfers between devices  49 us (27%)
  matrix products  28.6 us (16%)
  blocking collectives  16.6 us (9%)
  starting transfers between devices  15.5 us (8%)
  other arithmetic  7.52 us (4%)
  local copies, waits for them, and re-layouts  5.15 us (3%)
    pallas_call x1, Pallas kernels, rs_call(): pl.pallas_call(functools.partial(rs_kernel, tree), out_shape=jax.ShapeDty...  58.6 us
    all_to_all x1, waiting for transfers between devices, body(): block_heads = lax.all_to_all(heads, 'dp', 0, 0, tiled=True)  47 us
    all_to_all x3, blocking collectives, sent_to_all(): lax.all_to_all(jnp.broadcast_to(value[None], (devices, *value.shape)), ax...  12.1 us
    all_to_all x1, starting transfers between devices, body(): block_heads = lax.all_to_all(heads, 'dp', 0, 0, tiled=True)  11.9 us
    dot_general x2, matrix products, norm_layer(): pre_act = jnp.dot(normed, weight, preferred_element_type=jnp.float32)  9.12 us
    dot_general x1, matrix products, body(): lax.dot_general(spread, block_heads, (((0, 1), (0, 1)), ((), ())), prefer...  8.39 us
    dot_general x1, matrix products, body(): lax.dot_general(block_heads, hidden_top, (((2,), (1,)), ((), ())), prefer...  7.55 us
    all_to_all x1, blocking collectives, sum_at_owner(): lax.all_to_all(tiles, axis, split_axis=0, concat_axis=0, tiled=True)  4.58 us
  transfers between devices with their start and end apart: 2, of which 2 were waited for; matrix products, arithmetic and copies ran while one was open for 4% of the time, Pallas kernels for 0%

commit v1 on v0

v1 whole, which is shorter than its diff:
```python
import functools
import math

import jax
import jax.numpy as jnp
from jax import lax
from jax.experimental import pallas as pl
from jax.experimental.pallas import tpu as pltpu
from jax.sharding import PartitionSpec as P

EPSILON = 1e-06
MESH = pl.DeviceIdType.MESH
STRIDES = (16, 4, 1)
WIDTHS = ((384, 256, 384), (384, 384, 256))
STARTS = tuple(tuple(sum(w[:k]) for k in range(3)) for w in WIDTHS)
UNITS = (32, 8, 2)

def blend(core, a, b):
    return a + core * (b - a)

class Ring:
    def __init__(self, me, core, bufs):
        self.me, self.core = me, core
        self.g, self.t1, self.t2, self.rx, self.tx, self.ssem, self.rsem = bufs
        self.coords = tuple((me // s) % 4 for s in STRIDES)

    def dim(self, c, ph):
        k0, k1 = (c + ph) % 3, (c + ph + 1) % 3
        stride = blend(self.core, STRIDES[k0], STRIDES[k1])
        p = blend(self.core, self.coords[k0], self.coords[k1])
        right = self.me + ((p + 1) % 4 - p) * stride
        left = self.me + ((p + 3) % 4 - p) * stride
        return p, right, left

    def src(self, l, c, ph):
        return (self.g, self.t1, self.t2)[ph][l * 3 + c]

    def copy(self, l, c, ph, k, src, to):
        n = l * 3 + c
        return pltpu.make_async_remote_copy(
            src_ref=src, dst_ref=self.rx[ph][n].at[k],
            send_sem=self.ssem.at[n, ph, k], recv_sem=self.rsem.at[n, ph, k],
            device_id=(to, self.core), device_id_type=MESH)

    def copies(self, l, c, ph):
        p, right, left = self.dim(c, ph)
        P, H, tx = self.src(l, c, ph), UNITS[ph] // 2, self.tx[ph][l * 3 + c]
        half = (pl.ds(0, H), pl.ds(H, H))
        def nth(k):
            if k < 4:
                src = P.at[(p + (2, 1, 2, 3)[k]) % 4, half[(0, 1, 1, 0)[k]]]
            else:
                src = tx.at[k - 4]
            return self.copy(l, c, ph, k, src, (right, right, left, left, right, left)[k])
        return nth

    def start_a(self, l, c, ph):
        cp = self.copies(l, c, ph)
        for k in (0, 2, 1, 3):
            cp(k).start()

    def step_b(self, l, c, ph):
        cp = self.copies(l, c, ph)
        p, _, _ = self.dim(c, ph)
        P, H = self.src(l, c, ph), UNITS[ph] // 2
        rx, tx = self.rx[ph][l * 3 + c], self.tx[ph][l * 3 + c]
        for k, q, off in ((0, (p + 1) % 4, 0), (2, (p + 3) % 4, H)):
            cp(k).wait_recv()
            def add(u, n):
                tx[k // 2, pl.ds(u, n)] = (P[q, pl.ds(off + u, n)].astype(jnp.float32) + rx[k, pl.ds(u, n)].astype(jnp.float32)).astype(jnp.bfloat16)
            self.each(H, add)
            cp(4 + k // 2).start()

    def finish(self, l, c, ph, store):
        cp = self.copies(l, c, ph)
        p, _, _ = self.dim(c, ph)
        P, H = self.src(l, c, ph), UNITS[ph] // 2
        rx = self.rx[ph][l * 3 + c]
        for a, b, off in ((3, 4, 0), (1, 5, H)):
            cp(a).wait_recv()
            cp(b).wait_recv()
            def add(u, n):
                store(off + u, n, P[p, pl.ds(off + u, n)].astype(jnp.float32) + rx[a, pl.ds(u, n)].astype(jnp.float32) + rx[b, pl.ds(u, n)].astype(jnp.float32))
            self.each(H, add)

    @staticmethod
    def each(count, f):
        n = min(count, 4)
        if count == n:
            f(0, n)
        else:
            def body(i, c):
                f(pl.multiple_of(i * n, n), n)
                return c
            lax.fori_loop(0, count // n, body, 0)

    def next_phase(self, l, c, ph):
        t = (self.t1, self.t2)[ph][l * 3 + c]
        per = UNITS[ph + 1]
        def store(u, n, v):
            m = min(n, per)
            for j in range(0, n, m):
                q, r = (u + j) // per, (u + j) % per
                t[q, pl.ds(r, m)] = v[j:j + m].astype(jnp.bfloat16)
        self.finish(l, c, ph, store)
        self.start_a(l, c, ph + 1)

    def last(self, l, c, out):
        w0, w = STARTS[l][c], WIDTHS[l][c]
        def store(u, n, v):
            for j in range(n):
                out[l, (u + j) * 16:(u + j + 1) * 16, w0:w0 + w] = v[j]
        self.finish(l, c, 2, store)

    def put_partial(self, l, x, z, y, val):
        xyz = (x, z, y)
        v = val.astype(jnp.bfloat16).reshape(2, 16, 1024)
        for c in range(3):
            a, b, d = (blend(self.core, xyz[(c + k) % 3], xyz[(c + k + 1) % 3]) for k in range(3))
            w0, w = STARTS[l][c], WIDTHS[l][c]
            self.g[l * 3 + c][a, pl.ds((b * 4 + d) * 2, 2)] = v[:, :, w0:w0 + w]

    def wait_sends(self):
        for l in range(2):
            for c in range(3):
                for ph in range(3):
                    for k in range(6):
                        self.copies(l, c, ph)(k).wait_send()

def scratch():
    lc = [(l, c) for l in range(2) for c in range(3)]
    bf = jnp.bfloat16
    return [
        [pltpu.VMEM((4, 32, 16, WIDTHS[l][c]), bf) for l, c in lc],
        [pltpu.VMEM((4, 8, 16, WIDTHS[l][c]), bf) for l, c in lc],
        [pltpu.VMEM((4, 2, 16, WIDTHS[l][c]), bf) for l, c in lc],
        [[pltpu.VMEM((6, n // 2, 16, WIDTHS[l][c]), bf) for l, c in lc] for n in UNITS],
        [[pltpu.VMEM((2, n // 2, 16, WIDTHS[l][c]), bf) for l, c in lc] for n in UNITS],
        pltpu.SemaphoreType.DMA((6, 3, 6)),
        pltpu.SemaphoreType.DMA((6, 3, 6)),
    ]

def flat(tree):
    return jax.tree.flatten(tree, is_leaf=lambda v: not isinstance(v, list))

def partials(ring, l, nt_ref, delta_ref):
    def group(i, carry):
        rows = pl.ds(pl.multiple_of(i * 256, 256), 256)
        prod = jnp.dot(nt_ref[l, rows, :], delta_ref[l], preferred_element_type=jnp.float32)
        for k in range(8):
            ring.put_partial(l, i // 2, (i % 2) * 2 + k // 4, k % 4, prod[k * 32 : k * 32 + 32])
        return carry

    lax.fori_loop(0, 8, group, 0)


class Scatter:
    def __init__(self, ring, heads, bufs):
        self.ring, self.core, self.heads = ring, ring.core, heads
        self.r, self.f, self.ssem, self.rsem, self.lsem = bufs

    def piece(self, n, ph, q, j, m):
        h, c = n // 3, n % 3
        if ph == 0:
            w0, w = STARTS[h][c], WIDTHS[h][c]
            at = [slice(None)] * 3
            at[(c + m) % 3] = q
            at[(c + m + 1) % 3] = j
            return self.heads.at[(*at, h, slice(None), pl.ds(w0, w))]
        if ph == 1:
            return self.r[0][n].at[q, :, j]
        return self.r[1][n].at[q, j]

    def place(self, n, ph, j, s):
        return self.r[2][n].at[s, j] if ph == 2 else self.r[ph][n].at[j, s]

    def whole(self, n, ph, k):
        return self.r[ph][n].at[0] if k in (1, 3) else self.f[ph][n].at[0]

    def remote(self, n, ph, k, src, dst, to):
        return pltpu.make_async_remote_copy(
            src_ref=src,
            dst_ref=dst,
            send_sem=self.ssem.at[n, ph, k],
            recv_sem=self.rsem.at[n, ph, k],
            device_id=(to, self.core),
            device_id_type=MESH,
        )

    def on_core(self, ph, f):
        if ph:
            f(0)
        else:
            for m in range(2):
                pl.when(self.core == m)(functools.partial(f, m))

    def start(self, h, ph):
        def go(m):
            for c in range(3):
                n = h * 3 + c
                p, right, left = self.ring.dim(c, ph)
                f = self.f[ph][n]
                opposite = (p + 2) % 4
                for i in range(2):
                    self.remote(n, ph, 0, self.piece(n, ph, opposite, i, m), f.at[0, i], right).start()
                    self.remote(n, ph, 2, self.piece(n, ph, opposite, 2 + i, m), f.at[1, i], left).start()
                for j in range(4):
                    self.remote(
                        n, ph, 1, self.piece(n, ph, (p + 1) % 4, j, m), self.place(n, ph, j, p), right
                    ).start()
                    self.remote(
                        n, ph, 3, self.piece(n, ph, (p + 3) % 4, j, m), self.place(n, ph, j, p), left
                    ).start()
                for j in range(4):
                    pltpu.make_async_copy(
                        self.piece(n, ph, p, j, m), self.place(n, ph, j, p), self.lsem.at[n, ph]
                    ).start()

        self.on_core(ph, go)

    def wait(self, n, ph, k, sem):
        ref = self.whole(n, ph, k)
        pltpu.make_async_copy(ref, ref, sem).wait()

    def relay(self, h, ph):
        for c in range(3):
            n = h * 3 + c
            p, right, left = self.ring.dim(c, ph)
            f = self.f[ph][n]
            self.wait(n, ph, 0, self.rsem.at[n, ph, 0])
            for i in range(2):
                self.remote(n, ph, 4, f.at[0, i], self.place(n, ph, i, (p + 3) % 4), right).start()
            self.wait(n, ph, 2, self.rsem.at[n, ph, 2])
            for i in range(2):
                self.remote(n, ph, 5, f.at[1, i], self.place(n, ph, 2 + i, (p + 1) % 4), left).start()

    def finish(self, h, ph):
        for c in range(3):
            n = h * 3 + c
            self.wait(n, ph, 1, self.lsem.at[n, ph])
            for k in (1, 3, 4, 5):
                self.wait(n, ph, k, self.rsem.at[n, ph, k])

    def wait_sends(self):
        for n in range(6):
            for ph in range(3):
                for k in range(6):
                    self.wait(n, ph, k, self.ssem.at[n, ph, k])

    def owners_of(self, c):
        return tuple(
            blend(self.core, STRIDES[(c + k) % 3], STRIDES[(c + k + 1) % 3]) for k in range(3)
        )


def scatter_scratch():
    hc = [(h, c) for h in range(2) for c in range(3)]
    bf = jnp.bfloat16
    return [
        [[pltpu.VMEM((4, 4, 4, 16, WIDTHS[h][c]), bf) for h, c in hc] for _ in range(3)],
        [[pltpu.VMEM((2, 2, 4, 16, WIDTHS[h][c]), bf) for h, c in hc] for _ in range(3)],
        pltpu.SemaphoreType.DMA((6, 3, 6)),
        pltpu.SemaphoreType.DMA((6, 3, 6)),
        pltpu.SemaphoreType.DMA((6, 3)),
    ]


LIVE = 256
HALF = 1024
FULL = 2048
C0 = math.sqrt(2 / math.pi)
C1 = 0.044715


def work_scratch():
    f32, bf = jnp.float32, jnp.bfloat16
    return [
        pltpu.VMEM((2, FULL, HALF), bf),
        [pltpu.VMEM((2, LIVE, HALF), bf) for _ in range(2)],
        pltpu.VMEM((LIVE, HALF), bf),
        pltpu.VMEM((LIVE, FULL), bf),
        pltpu.VMEM((2, FULL, LIVE), bf),
        pltpu.VMEM((LIVE, 128), f32),
        pltpu.VMEM((2, LIVE, HALF), f32),
        pltpu.VMEM((LIVE, HALF), f32),
        pltpu.VMEM((LIVE, HALF), f32),
        pltpu.VMEM((2, LIVE, HALF), bf),
        pltpu.VMEM((2, 32, LIVE), f32),
        pltpu.VMEM((LIVE, 128), f32),
        pltpu.VMEM((LIVE, HALF), bf),
        pltpu.VMEM((2, LIVE, 128), f32),
        pltpu.VMEM((2, 4, LIVE, 256), bf),
        pltpu.VMEM((4, LIVE, 256), f32),
        pltpu.SemaphoreType.DMA((4,)),
        pltpu.SemaphoreType.DMA((8,)),
        pltpu.SemaphoreType.DMA((8,)),
    ]


def loop(count, f):
    def go(i, carry):
        f(i)
        return carry

    lax.fori_loop(0, count, go, 0)


def mega_kernel(tree, feats, gains, weights, heads, lengths, owners, labels, grads, loss, *refs):
    me, core = lax.axis_index("dp"), lax.axis_index("mp")
    ring_bufs, scatter_bufs, work = jax.tree.unflatten(tree, refs)
    (wts, xs, x2, nrm, nrm_t, r1, dgelu, pre1, up, delta, logit, owner_down, spread, stat, dn, dn_own, lsem, ssem, rsem) = work
    ring = Ring(me, core, ring_bufs)
    scatter = Scatter(ring, heads, scatter_bufs)
    other = 1 - core
    f32, bf = jnp.float32, jnp.bfloat16

    load = [pltpu.make_async_copy(weights.at[l], wts.at[l], lsem.at[l]) for l in range(2)]
    own_x = pltpu.make_async_copy(feats.at[pl.ds(0, LIVE)], xs[0].at[core], lsem.at[2])
    own_x.start()
    for cp in load:
        cp.start()

    def swap(k, src, dst):
        return pltpu.make_async_remote_copy(
            src_ref=src,
            dst_ref=dst,
            send_sem=ssem.at[k],
            recv_sem=rsem.at[k],
            device_id=(me, other),
            device_id_type=MESH,
        )

    bar = pltpu.get_barrier_semaphore()
    pl.semaphore_signal(bar, inc=1, device_id=(me, other), device_id_type=MESH)
    for s in STRIDES:
        p = (me // s) % 4
        for step in (1, 3):
            to = me + ((p + step) % 4 - p) * s
            pl.semaphore_signal(bar, inc=1, device_id=(to, core), device_id_type=MESH)
    pl.semaphore_wait(bar, 7)

    swap_x = [swap(0, feats.at[pl.ds(0, LIVE)], xs[0].at[core]), swap(1, xs[1].at[core], xs[1].at[core])]
    swap_x[0].start()
    for h in range(2):
        scatter.start(h, 0)

    def down(row):
        same = lax.broadcasted_iota(jnp.int32, (64, 64), 0) == lax.broadcasted_iota(jnp.int32, (64, 64), 1)
        return jnp.sum(jnp.where(same, row, 0), 1, keepdims=True)

    lens = lengths[...]
    upto = lax.broadcasted_iota(jnp.int32, (64, 64), 1) <= lax.broadcasted_iota(jnp.int32, (64, 64), 0)
    ends = jnp.sum(jnp.where(upto, lens, 0), 1, keepdims=True)
    lens_down = down(lens)
    slot = lax.broadcasted_iota(jnp.int32, (64, LIVE), 1)
    here = (slot < ends) & (slot >= ends - lens_down)
    slot_owner = jnp.sum(jnp.where(here, down(owners[...]), 0), 0, keepdims=True)
    slot_len = jnp.sum(jnp.where(here, lens_down, 0), 0, keepdims=True)
    owner_down[...] = jnp.broadcast_to(slot_owner.astype(f32), (128, LIVE)).T

    def layer(l):
        def norm(i):
            rows = pl.ds(pl.multiple_of(i * 32, 32), 32)
            a, b = xs[l][0, rows, :].astype(f32), xs[l][1, rows, :].astype(f32)
            mean = (jnp.sum(a * a, -1, keepdims=True) + jnp.sum(b * b, -1, keepdims=True)) * (1.0 / FULL)
            scale = lax.rsqrt(mean + EPSILON)
            nrm[rows, 0:HALF] = (a * scale * gains[l : l + 1, 0:HALF]).astype(bf)
            nrm[rows, HALF:FULL] = (b * scale * gains[l : l + 1, HALF:FULL]).astype(bf)
            if l == 1:
                r1[rows, :] = jnp.broadcast_to(scale, (32, 128))

        loop(LIVE // 32, norm)

        def columns(i):
            cols = pl.ds(pl.multiple_of(i * 256, 256), 256)
            pre = jnp.dot(nrm[...], wts[l, :, cols], preferred_element_type=f32)
            t = jnp.tanh(C0 * (pre + C1 * (pre * pre * pre)))
            half = 0.5 * (1.0 + t)
            dgelu[l, :, cols] = half + 0.5 * pre * (1.0 - t * t) * (C0 * (1.0 + 3.0 * C1 * (pre * pre)))
            out = (xs[l][core, :, cols].astype(f32) + pre * half).astype(bf)
            if l == 0:
                xs[1][core, :, cols] = out
            else:
                x2[:, cols] = out
                pre1[:, cols] = pre

        loop(HALF // 256, columns)
        if l == 0:
            swap_x[1].start()

        def turn(i):
            cols = pl.ds(pl.multiple_of(i * 256, 256), 256)
            nrm_t[l, cols, :] = nrm[:, cols].astype(f32).T.astype(bf)

        loop(FULL // 256, turn)

    own_x.wait()
    swap_x[0].wait_recv()
    load[0].wait()
    layer(0)
    scatter.relay(0, 0)
    swap_x[1].wait_recv()
    load[1].wait()
    layer(1)
    scatter.relay(1, 0)
    for ph in range(2):
        for h in range(2):
            scatter.finish(h, ph)
            scatter.start(h, ph + 1)
        for h in range(2):
            scatter.relay(h, ph + 1)

    for h in range(2):
        scatter.finish(h, 2)
        total = jnp.zeros((16, LIVE), f32)
        for c in range(3):
            w0, w = STARTS[h][c], WIDTHS[h][c]
            sa, sb, sc = scatter.owners_of(c)
            block = scatter.r[2][h * 3 + c]

            def pick(i, acc):
                part = block[i].reshape(256, w)
                prod = lax.dot_general(
                    part, x2[:, w0 : w0 + w], (((1,), (1,)), ((), ())), preferred_element_type=f32
                )
                for k in range(16):
                    owner = (k % 4) * sa + (k // 4) * sb + i * sc
                    acc = acc + jnp.where(slot_owner == owner, prod[k * 16 : k * 16 + 16], 0.0)
                return acc

            total = lax.fori_loop(0, 4, pick, total)
        logit[0, 16 * h : 16 * h + 16, :] = total
    swap_logit = swap(2, logit.at[0], logit.at[1])
    swap_logit.start()
    swap_logit.wait_recv()
    scores = logit[0] + logit[1]
    hit = lax.broadcasted_iota(jnp.int32, (32, LIVE), 0) == labels[0:1, 0:LIVE]
    log_total = jnp.log(jnp.sum(jnp.exp(scores), 0, keepdims=True))
    picked = jnp.sum(jnp.where(hit, scores, 0.0), 0, keepdims=True)
    loss[0:1, 0:LIVE] = (log_total - picked).astype(bf)
    loss[0:1, LIVE : 2 * LIVE] = jnp.zeros((1, LIVE), bf)
    dlogits = (jnp.exp(scores - log_total) - hit.astype(f32)) * (1.0 / slot_len.astype(f32))

    group = lax.broadcasted_iota(jnp.int32, (1, 128), 1) // 16
    for h in range(2):
        tiled = jnp.concatenate([dlogits[16 * h : 16 * h + 16]] * 8, axis=0).T
        for c in range(3):
            w0, w = STARTS[h][c], WIDTHS[h][c]
            sa, sb, sc = scatter.owners_of(c)
            for j in range(8):
                owner = (group % 4) * sa + (2 * (j % 2) + group // 4) * sb + (j // 2) * sc
                spread[:, 128 * j : 128 * j + 128] = jnp.where(
                    owner_down[...] == owner.astype(f32), tiled, 0.0
                ).astype(bf)
            block = scatter.r[2][h * 3 + c]
            grad = jnp.dot(spread[...], block[...].reshape(1024, w), preferred_element_type=f32)
            cols = slice(w0, w0 + w)
            up[:, cols] = grad if h == 0 else up[:, cols] + grad

    def back(i):
        rows = pl.ds(pl.multiple_of(i * 32, 32), 32)
        u = up[rows, :].astype(bf).astype(f32)
        up[rows, :] = u
        d = (u * dgelu[1, rows, :]).astype(bf)
        delta[1, rows, :] = d
        row = jnp.sum(d.astype(f32) * pre1[rows, :], -1, keepdims=True)
        stat[0, rows, :] = jnp.broadcast_to(row, (32, 128)) / r1[rows, :]

    loop(LIVE // 32, back)
    swap_stat = swap(3, stat.at[0], stat.at[1])
    swap_stat.start()

    def begin(l):
        partials(ring, l, nrm_t, delta)
        for c in range(3):
            ring.start_a(l, c, 0)

    begin(1)
    swap_dn = [swap(4 + i, dn.at[0, i], dn.at[1, i]) for i in range(4)]
    for i in range(4):
        part = wts[1, pl.ds(pl.multiple_of(other * HALF + i * 256, 256), 256), :]
        dn[0, i] = lax.dot_general(
            delta[1], part, (((1,), (1,)), ((), ())), preferred_element_type=f32
        ).astype(bf)
        swap_dn[i].start()

    def own_part(i):
        part = wts[1, pl.ds(pl.multiple_of(core * HALF + i * 256, 256), 256), :]
        dn_own[i] = lax.dot_general(delta[1], part, (((1,), (1,)), ((), ())), preferred_element_type=f32)

    loop(4, own_part)
    swap_stat.wait_recv()
    for i in range(4):
        swap_dn[i].wait_recv()
        cols = slice(256 * i, 256 * i + 256)
        gain = jnp.where(core == 0, gains[1:2, 256 * i : 256 * i + 256], gains[1:2, HALF + 256 * i : HALF + 256 * i + 256])

        def dx(k):
            rows = pl.ds(pl.multiple_of(k * 64, 64), 64)
            scale = r1[rows, 0:1]
            cross = (stat[0, rows, 0:1] + stat[1, rows, 0:1]) * (1.0 / FULL)
            d = (
                up[rows, cols]
                + gain * scale * (dn_own[i, rows, :] + dn[1, i, rows, :].astype(f32))
                - xs[1][core, rows, cols].astype(f32) * (scale * scale * scale * cross)
            )
            delta[0, rows, cols] = (d * dgelu[0, rows, cols]).astype(bf)

        loop(LIVE // 64, dx)
    begin(0)
    for ph in range(3):
        for l in (1, 0):
            for c in range(3):
                ring.step_b(l, c, ph)
        for l in (1, 0):
            for c in range(3):
                if ph < 2:
                    ring.next_phase(l, c, ph)
                else:
                    ring.last(l, c, grads)
    ring.wait_sends()
    scatter.wait_sends()
    for cp in (*swap_x, swap_logit, swap_stat, *swap_dn):
        cp.wait_send()


def body(features, gains, weights, heads, lengths, owners, labels):
    slots = features.shape[0]
    leaves, tree = flat([scratch(), scatter_scratch(), work_scratch()])
    vmem, hbm = pl.BlockSpec(memory_space=pltpu.VMEM), pl.BlockSpec(memory_space=pl.ANY)
    grads, loss = pl.pallas_call(
        functools.partial(mega_kernel, tree),
        out_shape=(
            jax.ShapeDtypeStruct((2, 32, HALF), jnp.float32),
            jax.ShapeDtypeStruct((1, slots), jnp.bfloat16),
        ),
        in_specs=[hbm, vmem, hbm, hbm, vmem, vmem, vmem],
        out_specs=(vmem, vmem),
        scratch_shapes=leaves,
        compiler_params=pltpu.CompilerParams(
            collective_id=0, has_side_effects=True, vmem_limit_bytes=67043328
        ),
        name="step",
    )(
        features,
        gains,
        weights,
        heads.reshape(4, 4, 4, 2, 16, HALF),
        lengths,
        owners,
        labels.reshape(1, slots),
    )
    return (grads, loss.reshape(slots))


def solution(mesh):
    return jax.shard_map(
        body,
        mesh=mesh,
        in_specs=(
            P("dp", "mp"),
            P(),
            P(None, None, "mp"),
            P("dp", None, "mp"),
            P("dp", None),
            P("dp", None),
            P("dp"),
        ),
        out_specs=(P(None, "dp", "mp"), P("dp")),
        check_vma=False,
    )
```

time: 183 us -> 119 us (0.65)
  Pallas kernels: 58.6 us -> 115 us
  waiting for transfers between devices: 49 us -> 0 us
  matrix products: 28.6 us -> 0 us
  blocking collectives: 16.6 us -> 0 us
  starting transfers between devices: 15.5 us -> 0 us
  other arithmetic: 7.52 us -> 1.25 us
  local copies, waits for them, and re-layouts: 5.15 us -> 1.67 us
    pallas_call x1, Pallas kernels: 58.6 us -> 115 us  [body(): pl.pallas_call(functools.partial(mega_kernel, tree), out_shape=(jax.Shape...]
    all_to_all x2 -> x0, waiting for transfers between devices: 49 us -> none  [the longest x1 47 us: body(): block_heads = lax.all_to_all(heads, 'dp', 0, 0, tiled=True)]
    dot_general x5 -> x0, matrix products: 28.6 us -> none  [the longest x2 9.12 us: norm_layer(): pre_act = jnp.dot(normed, weight, preferred_element_type=jnp.float32)]
    all_to_all x4 -> x0, blocking collectives: 16.6 us -> none  [the longest x3 12.1 us: sent_to_all(): lax.all_to_all(jnp.broadcast_to(value[None], (devices, *value.shape)), ax...]
    all_to_all x2 -> x0, starting transfers between devices: 15.5 us -> none  [the longest x1 11.9 us: body(): block_heads = lax.all_to_all(heads, 'dp', 0, 0, tiled=True)]
    another operation x7 -> x0, other arithmetic: 5.55 us -> none  [the longest x2 3.15 us: body(): jnp.stack([delta_first, delta_second])]
  transfers between devices with their start and end apart: 2 -> 0, of which waited for: 2 -> 0; matrix products, arithmetic and copies ran while one was open for 4% -> 0% of each run, Pallas kernels for 0% -> 0%
where the time goes in v1:
time: 119 us
  Pallas kernels  115 us (97%)
  local copies, waits for them, and re-layouts  1.67 us (1%)
  other arithmetic  1.25 us (1%)
    pallas_call x1, Pallas kernels, body(): pl.pallas_call(functools.partial(mega_kernel, tree), out_shape=(jax.Shape...  115 us

profile of v1, /device:TPU:0, one launch (start us, length us, event | category | flops | bytes accessed | tf_op | source)
XLA Modules:
  0.0 118.8 jit_solution(549518383725923279)
XLA Ops:
  0.6 115.3 %step.1 = (f32[2,32,1024]{2,1,0:T(8,128)}, bf16[1,512]{1,0:T(2,128)(2,1)}) custom-call(bf16[512,1024]{1,0:T(8,128)(2,1)} %feats.1, f32[2,2048]{1,0:T(2,128)} %gains.1, bf16[2,2048,1024]{2,1,0:T(8,128)(2,1)} %weights.1, bf16[4,4,4,2,16,1024]{5,4,3,2,1,0:T(8,128)(2,1)} %bitcast.2, s32[1,64]{1,0:T(1,128)} %lengths.1, s32[1,64]{1,0:T(1,128)} %owners.1, ...), custom_call_target="tpu_custom_call" | custom-call | tf_op jit(solution)/shard_map/step/pallas_call | solution.py:531
  115.9 1.2 %reduce = bf16[512]{0:T(512)(128)(2,1)} reduce(bf16[1,512]{1,0:T(2,128)(2,1)} %get-tuple-element.5, bf16[]{:T(256)} %constant.2), dimensions={0}, to_apply=%get-tuple-element.5.reduce_sub_computation | reduce | bytes 2050 | tf_op jit(solution)/shard_map/step/pallas_call | solution.py:531
  117.1 1.7 %copy.10 = f32[2,32,1024]{2,1,0:T(8,128)} copy(f32[2,32,1024]{2,1,0:T(8,128)} %get-tuple-element.8) | data formatting | bytes 524288

commit v2 on v1

--- a/solution.py
+++ b/solution.py
@@ -13,7 +13,7 @@
 STRIDES = (16, 4, 1)
 WIDTHS = ((384, 256, 384), (384, 384, 256))
 STARTS = tuple(tuple(sum(w[:k]) for k in range(3)) for w in WIDTHS)
-UNITS = (32, 8, 2)
+UNITS = (16, 4, 1)
 
 def blend(core, a, b):
     return a + core * (b - a)
@@ -32,56 +32,95 @@
         left = self.me + ((p + 3) % 4 - p) * stride
         return p, right, left
 
-    def src(self, l, c, ph):
-        return (self.g, self.t1, self.t2)[ph][l * 3 + c]
-
-    def copy(self, l, c, ph, k, src, to):
-        n = l * 3 + c
-        return pltpu.make_async_remote_copy(
-            src_ref=src, dst_ref=self.rx[ph][n].at[k],
-            send_sem=self.ssem.at[n, ph, k], recv_sem=self.rsem.at[n, ph, k],
-            device_id=(to, self.core), device_id_type=MESH)
-
-    def copies(self, l, c, ph):
+    def copies(self, k, c, ph):
         p, right, left = self.dim(c, ph)
-        P, H, tx = self.src(l, c, ph), UNITS[ph] // 2, self.tx[ph][l * 3 + c]
-        half = (pl.ds(0, H), pl.ds(H, H))
-        def nth(k):
-            if k < 4:
-                src = P.at[(p + (2, 1, 2, 3)[k]) % 4, half[(0, 1, 1, 0)[k]]]
+        n = k * 3 + c
+        part = (self.g, self.t1, self.t2)[ph][n]
+        half = UNITS[ph] // 2
+        lo, hi = pl.ds(0, half), pl.ds(half, half)
+
+        def nth(i):
+            if ph == 2:
+                src = part.at[(p + (1, 3, 2)[i]) % 4]
+                stride = blend(self.core, STRIDES[(c + 2) % 3], STRIDES[c])
+                to = (right, left, self.me + ((p + 2) % 4 - p) * stride)[i]
+            elif i < 4:
+                src = part.at[(p + (2, 1, 2, 3)[i]) % 4, (lo, hi, hi, lo)[i]]
+                to = (right, right, left, left)[i]
             else:
-                src = tx.at[k - 4]
-            return self.copy(l, c, ph, k, src, (right, right, left, left, right, left)[k])
+                src = self.tx[ph][n].at[i - 4]
+                to = (right, left)[i - 4]
+            return pltpu.make_async_remote_copy(
+                src_ref=src,
+                dst_ref=self.rx[ph][n].at[i],
+                send_sem=self.ssem.at[n, ph, i],
+                recv_sem=self.rsem.at[n, ph, i],
+                device_id=(to, self.core),
+                device_id_type=MESH,
+            )
+
         return nth
 
-    def start_a(self, l, c, ph):
-        cp = self.copies(l, c, ph)
-        for k in (0, 2, 1, 3):
-            cp(k).start()
-
-    def step_b(self, l, c, ph):
-        cp = self.copies(l, c, ph)
-        p, _, _ = self.dim(c, ph)
-        P, H = self.src(l, c, ph), UNITS[ph] // 2
-        rx, tx = self.rx[ph][l * 3 + c], self.tx[ph][l * 3 + c]
-        for k, q, off in ((0, (p + 1) % 4, 0), (2, (p + 3) % 4, H)):
-            cp(k).wait_recv()
-            def add(u, n):
-                tx[k // 2, pl.ds(u, n)] = (P[q, pl.ds(off + u, n)].astype(jnp.float32) + rx[k, pl.ds(u, n)].astype(jnp.float32)).astype(jnp.bfloat16)
-            self.each(H, add)
-            cp(4 + k // 2).start()
-
-    def finish(self, l, c, ph, store):
-        cp = self.copies(l, c, ph)
-        p, _, _ = self.dim(c, ph)
-        P, H = self.src(l, c, ph), UNITS[ph] // 2
-        rx = self.rx[ph][l * 3 + c]
-        for a, b, off in ((3, 4, 0), (1, 5, H)):
-            cp(a).wait_recv()
-            cp(b).wait_recv()
-            def add(u, n):
-                store(off + u, n, P[p, pl.ds(off + u, n)].astype(jnp.float32) + rx[a, pl.ds(u, n)].astype(jnp.float32) + rx[b, pl.ds(u, n)].astype(jnp.float32))
-            self.each(H, add)
+    def start(self, k, c, ph):
+        cp = self.copies(k, c, ph)
+        for i in (0, 1, 2) if ph == 2 else (0, 2, 1, 3):
+            cp(i).start()
+
+    def forward(self, k, ph):
+        half = UNITS[ph] // 2
+        for c in range(3):
+            n = k * 3 + c
+            cp = self.copies(k, c, ph)
+            p, _, _ = self.dim(c, ph)
+            part, rx, tx = (self.g, self.t1)[ph][n], self.rx[ph][n], self.tx[ph][n]
+            for i, q, off in ((0, (p + 1) % 4, 0), (2, (p + 3) % 4, half)):
+                cp(i).wait_recv()
+
+                def add(u, m):
+                    tx[i // 2, pl.ds(u, m)] = (
+                        part[q, pl.ds(off + u, m)].astype(jnp.float32)
+                        + rx[i, pl.ds(u, m)].astype(jnp.float32)
+                    ).astype(jnp.bfloat16)
+
+                self.each(half, add)
+                cp(4 + i // 2).start()
+
+    def finish(self, k, ph):
+        half, per = UNITS[ph] // 2, UNITS[ph + 1]
+        for c in range(3):
+            n = k * 3 + c
+            cp = self.copies(k, c, ph)
+            p, _, _ = self.dim(c, ph)
+            part, rx, t = (self.g, self.t1)[ph][n], self.rx[ph][n], (self.t1, self.t2)[ph][n]
+            for a, b, off in ((3, 4, 0), (1, 5, half)):
+                cp(a).wait_recv()
+                cp(b).wait_recv()
+
+                def add(u, m):
+                    v = (
+                        part[p, pl.ds(off + u, m)].astype(jnp.float32)
+                        + rx[a, pl.ds(u, m)].astype(jnp.float32)
+                        + rx[b, pl.ds(u, m)].astype(jnp.float32)
+                    ).astype(jnp.bfloat16)
+                    for q in range(m // per):
+                        t[(off + u) // per + q] = v[q * per : (q + 1) * per]
+
+                self.each(half, add)
+            self.start(k, c, ph + 1)
+
+    def last(self, k, out):
+        l, r = k // 2, k % 2
+        for c in range(3):
+            n = k * 3 + c
+            cp = self.copies(k, c, 2)
+            p, _, _ = self.dim(c, 2)
+            for i in range(3):
+                cp(i).wait_recv()
+            total = self.t2[n][p, 0].astype(jnp.float32)
+            for i in range(3):
+                total = total + self.rx[2][n][i, 0].astype(jnp.float32)
+            w0, w = STARTS[l][c], WIDTHS[l][c]
+            out[l, 16 * r : 16 * r + 16, w0 : w0 + w] = total
 
     @staticmethod
     def each(count, f):
@@ -89,69 +128,59 @@
         if count == n:
             f(0, n)
         else:
-            def body(i, c):
+
+            def go(i, carry):
                 f(pl.multiple_of(i * n, n), n)
-                return c
-            lax.fori_loop(0, count // n, body, 0)
-
-    def next_phase(self, l, c, ph):
-        t = (self.t1, self.t2)[ph][l * 3 + c]
-        per = UNITS[ph + 1]
-        def store(u, n, v):
-            m = min(n, per)
-            for j in range(0, n, m):
-                q, r = (u + j) // per, (u + j) % per
-                t[q, pl.ds(r, m)] = v[j:j + m].astype(jnp.bfloat16)
-        self.finish(l, c, ph, store)
-        self.start_a(l, c, ph + 1)
-
-    def last(self, l, c, out):
-        w0, w = STARTS[l][c], WIDTHS[l][c]
-        def store(u, n, v):
-            for j in range(n):
-                out[l, (u + j) * 16:(u + j + 1) * 16, w0:w0 + w] = v[j]
-        self.finish(l, c, 2, store)
-
-    def put_partial(self, l, x, z, y, val):
-        xyz = (x, z, y)
-        v = val.astype(jnp.bfloat16).reshape(2, 16, 1024)
-        for c in range(3):
-            a, b, d = (blend(self.core, xyz[(c + k) % 3], xyz[(c + k + 1) % 3]) for k in range(3))
-            w0, w = STARTS[l][c], WIDTHS[l][c]
-            self.g[l * 3 + c][a, pl.ds((b * 4 + d) * 2, 2)] = v[:, :, w0:w0 + w]
+                return carry
+
+            lax.fori_loop(0, count // n, go, 0)
 
     def wait_sends(self):
-        for l in range(2):
+        for k in range(4):
             for c in range(3):
                 for ph in range(3):
-                    for k in range(6):
-                        self.copies(l, c, ph)(k).wait_send()
-
-def scratch():
-    lc = [(l, c) for l in range(2) for c in range(3)]
+                    for i in range(3 if ph == 2 else 6):
+                        self.copies(k, c, ph)(i).wait_send()
+
+
+def ring_scratch():
     bf = jnp.bfloat16
+    widths = [WIDTHS[k // 2][c] for k in range(4) for c in range(3)]
     return [
-        [pltpu.VMEM((4, 32, 16, WIDTHS[l][c]), bf) for l, c in lc],
-        [pltpu.VMEM((4, 8, 16, WIDTHS[l][c]), bf) for l, c in lc],
-        [pltpu.VMEM((4, 2, 16, WIDTHS[l][c]), bf) for l, c in lc],
-        [[pltpu.VMEM((6, n // 2, 16, WIDTHS[l][c]), bf) for l, c in lc] for n in UNITS],
-        [[pltpu.VMEM((2, n // 2, 16, WIDTHS[l][c]), bf) for l, c in lc] for n in UNITS],
-        pltpu.SemaphoreType.DMA((6, 3, 6)),
-        pltpu.SemaphoreType.DMA((6, 3, 6)),
+        *[[pltpu.VMEM((4, n, 16, w), bf) for w in widths] for n in UNITS],
+        [[pltpu.VMEM((6, n // 2, 16, w) if n > 1 else (3, 1, 16, w), bf) for w in widths] for n in UNITS],
+        [[pltpu.VMEM((2, n // 2, 16, w), bf) for w in widths] for n in UNITS[:2]],
+        pltpu.SemaphoreType.DMA((12, 3, 6)),
+        pltpu.SemaphoreType.DMA((12, 3, 6)),
     ]
+
 
 def flat(tree):
     return jax.tree.flatten(tree, is_leaf=lambda v: not isinstance(v, list))
 
-def partials(ring, l, nt_ref, delta_ref):
-    def group(i, carry):
-        rows = pl.ds(pl.multiple_of(i * 256, 256), 256)
-        prod = jnp.dot(nt_ref[l, rows, :], delta_ref[l], preferred_element_type=jnp.float32)
-        for k in range(8):
-            ring.put_partial(l, i // 2, (i % 2) * 2 + k // 4, k % 4, prod[k * 32 : k * 32 + 32])
-        return carry
-
-    lax.fori_loop(0, 8, group, 0)
+
+def begin(ring, k, nt_ref, delta_ref):
+    l, r = k // 2, k % 2
+    for c in range(3):
+        w0, w = STARTS[l][c], WIDTHS[l][c]
+        g = ring.g[k * 3 + c]
+
+        def group(x, carry):
+            rows = pl.ds(pl.multiple_of(x * 256, 256), 256)
+            prod = jnp.dot(
+                nt_ref[l, r, rows, :], delta_ref[l, :, w0 : w0 + w], preferred_element_type=jnp.float32
+            )
+            v = prod.astype(jnp.bfloat16).reshape(16, 16, w)
+            for i in range(16):
+                xyz = (x, i // 4, i % 4)
+                a, b, d = (
+                    blend(ring.core, xyz[(c + e) % 3], xyz[(c + e + 1) % 3]) for e in range(3)
+                )
+                g[a, b * 4 + d] = v[i]
+            return carry
+
+        lax.fori_loop(0, 4, group, 0)
+        ring.start(k, c, 0)
 
 
 class Scatter:
@@ -279,7 +308,7 @@
         [pltpu.VMEM((2, LIVE, HALF), bf) for _ in range(2)],
         pltpu.VMEM((LIVE, HALF), bf),
         pltpu.VMEM((LIVE, FULL), bf),
-        pltpu.VMEM((2, FULL, LIVE), bf),
+        pltpu.VMEM((2, 2, HALF, LIVE), bf),
         pltpu.VMEM((LIVE, 128), f32),
         pltpu.VMEM((2, LIVE, HALF), f32),
         pltpu.VMEM((LIVE, HALF), f32),
@@ -291,7 +320,11 @@
         pltpu.VMEM((2, LIVE, 128), f32),
         pltpu.VMEM((2, 4, LIVE, 256), bf),
         pltpu.VMEM((4, LIVE, 256), f32),
-        pltpu.SemaphoreType.DMA((4,)),
+        pltpu.VMEM((2, FULL), f32),
+        pltpu.VMEM((1, 64), jnp.int32),
+        pltpu.VMEM((1, 64), jnp.int32),
+        pltpu.VMEM((1, 2 * LIVE), jnp.int32),
+        pltpu.SemaphoreType.DMA((8,)),
         pltpu.SemaphoreType.DMA((8,)),
         pltpu.SemaphoreType.DMA((8,)),
     ]
@@ -305,10 +338,10 @@
     lax.fori_loop(0, count, go, 0)
 
 
-def mega_kernel(tree, feats, gains, weights, heads, lengths, owners, labels, grads, loss, *refs):
+def mega_kernel(tree, feats, gains_hbm, weights, heads, lengths_hbm, owners_hbm, labels_hbm, grads, loss, *refs):
     me, core = lax.axis_index("dp"), lax.axis_index("mp")
     ring_bufs, scatter_bufs, work = jax.tree.unflatten(tree, refs)
-    (wts, xs, x2, nrm, nrm_t, r1, dgelu, pre1, up, delta, logit, owner_down, spread, stat, dn, dn_own, lsem, ssem, rsem) = work
+    (wts, xs, x2, nrm, nrm_t, r1, dgelu, pre1, up, delta, logit, owner_down, spread, stat, dn, dn_own, gains, lengths, owners, labels, lsem, ssem, rsem) = work
     ring = Ring(me, core, ring_bufs)
     scatter = Scatter(ring, heads, scatter_bufs)
     other = 1 - core
@@ -316,8 +349,13 @@
 
     load = [pltpu.make_async_copy(weights.at[l], wts.at[l], lsem.at[l]) for l in range(2)]
     own_x = pltpu.make_async_copy(feats.at[pl.ds(0, LIVE)], xs[0].at[core], lsem.at[2])
-    own_x.start()
-    for cp in load:
+    small = [
+        pltpu.make_async_copy(src, dst, lsem.at[3 + i])
+        for i, (src, dst) in enumerate(
+            ((gains_hbm, gains), (lengths_hbm, lengths), (owners_hbm, owners), (labels_hbm, labels))
+        )
+    ]
+    for cp in (own_x, *small, *load):
         cp.start()
 
     def swap(k, src, dst):
@@ -348,6 +386,8 @@
         same = lax.broadcasted_iota(jnp.int32, (64, 64), 0) == lax.broadcasted_iota(jnp.int32, (64, 64), 1)
         return jnp.sum(jnp.where(same, row, 0), 1, keepdims=True)
 
+    for cp in small:
+        cp.wait()
     lens = lengths[...]
     upto = lax.broadcasted_iota(jnp.int32, (64, 64), 1) <= lax.broadcasted_iota(jnp.int32, (64, 64), 0)
     ends = jnp.sum(jnp.where(upto, lens, 0), 1, keepdims=True)
@@ -358,7 +398,7 @@
     slot_len = jnp.sum(jnp.where(here, lens_down, 0), 0, keepdims=True)
     owner_down[...] = jnp.broadcast_to(slot_owner.astype(f32), (128, LIVE)).T
 
-    def layer(l):
+    def norm_layer(l):
         def norm(i):
             rows = pl.ds(pl.multiple_of(i * 32, 32), 32)
             a, b = xs[l][0, rows, :].astype(f32), xs[l][1, rows, :].astype(f32)
@@ -371,6 +411,7 @@
 
         loop(LIVE // 32, norm)
 
+    def main_layer(l):
         def columns(i):
             cols = pl.ds(pl.multiple_of(i * 256, 256), 256)
             pre = jnp.dot(nrm[...], wts[l, :, cols], preferred_element_type=f32)
@@ -388,27 +429,39 @@
         if l == 0:
             swap_x[1].start()
 
+    def turn_layer(l):
         def turn(i):
             cols = pl.ds(pl.multiple_of(i * 256, 256), 256)
-            nrm_t[l, cols, :] = nrm[:, cols].astype(f32).T.astype(bf)
+            turned = nrm[:, cols].astype(f32).T.astype(bf).reshape(8, 2, 16, LIVE)
+            for k in range(2):
+                nrm_t[l, k, pl.ds(pl.multiple_of(i * 128, 128), 128), :] = turned[:, k].reshape(128, LIVE)
 
         loop(FULL // 256, turn)
 
     own_x.wait()
     swap_x[0].wait_recv()
+    norm_layer(0)
     load[0].wait()
-    layer(0)
+    main_layer(0)
     scatter.relay(0, 0)
+    turn_layer(0)
     swap_x[1].wait_recv()
+    norm_layer(1)
+    scatter.relay(1, 0)
     load[1].wait()
-    layer(1)
-    scatter.relay(1, 0)
-    for ph in range(2):
-        for h in range(2):
-            scatter.finish(h, ph)
-            scatter.start(h, ph + 1)
-        for h in range(2):
-            scatter.relay(h, ph + 1)
+    main_layer(1)
+    scatter.finish(0, 0)
+    scatter.start(0, 1)
+    scatter.finish(1, 0)
+    scatter.start(1, 1)
+    turn_layer(1)
+    for h in range(2):
+        scatter.relay(h, 1)
+    for h in range(2):
+        scatter.finish(h, 1)
+        scatter.start(h, 2)
+    for h in range(2):
+        scatter.relay(h, 2)
 
     for h in range(2):
         scatter.finish(h, 2)
@@ -418,17 +471,15 @@
             sa, sb, sc = scatter.owners_of(c)
             block = scatter.r[2][h * 3 + c]
 
-            def pick(i, acc):
-                part = block[i].reshape(256, w)
-                prod = lax.dot_general(
-                    part, x2[:, w0 : w0 + w], (((1,), (1,)), ((), ())), preferred_element_type=f32
-                )
-                for k in range(16):
-                    owner = (k % 4) * sa + (k // 4) * sb + i * sc
-                    acc = acc + jnp.where(slot_owner == owner, prod[k * 16 : k * 16 + 16], 0.0)
-                return acc
-
-            total = lax.fori_loop(0, 4, pick, total)
+            prod = lax.dot_general(
+                block[...].reshape(1024, w),
+                x2[:, w0 : w0 + w],
+                (((1,), (1,)), ((), ())),
+                preferred_element_type=f32,
+            )
+            for k in range(64):
+                owner = (k % 4) * sa + (k // 4 % 4) * sb + (k // 16) * sc
+                total = total + jnp.where(slot_owner == owner, prod[k * 16 : k * 16 + 16], 0.0)
         logit[0, 16 * h : 16 * h + 16, :] = total
     swap_logit = swap(2, logit.at[0], logit.at[1])
     swap_logit.start()
@@ -437,8 +488,10 @@
     hit = lax.broadcasted_iota(jnp.int32, (32, LIVE), 0) == labels[0:1, 0:LIVE]
     log_total = jnp.log(jnp.sum(jnp.exp(scores), 0, keepdims=True))
     picked = jnp.sum(jnp.where(hit, scores, 0.0), 0, keepdims=True)
-    loss[0:1, 0:LIVE] = (log_total - picked).astype(bf)
-    loss[0:1, LIVE : 2 * LIVE] = jnp.zeros((1, LIVE), bf)
+    losses = (log_total - picked).astype(bf)
+    loss[0:1, :] = losses[:, 0:128]
+    loss[1:2, :] = losses[:, 128:LIVE]
+    loss[2:4, :] = jnp.zeros((2, 128), bf)
     dlogits = (jnp.exp(scores - log_total) - hit.astype(f32)) * (1.0 / slot_len.astype(f32))
 
     group = lax.broadcasted_iota(jnp.int32, (1, 128), 1) // 16
@@ -470,12 +523,8 @@
     swap_stat = swap(3, stat.at[0], stat.at[1])
     swap_stat.start()
 
-    def begin(l):
-        partials(ring, l, nrm_t, delta)
-        for c in range(3):
-            ring.start_a(l, c, 0)
-
-    begin(1)
+    for k in (2, 3):
+        begin(ring, k, nrm_t, delta)
     swap_dn = [swap(4 + i, dn.at[0, i], dn.at[1, i]) for i in range(4)]
     for i in range(4):
         part = wts[1, pl.ds(pl.multiple_of(other * HALF + i * 256, 256), 256), :]
@@ -483,6 +532,7 @@
             delta[1], part, (((1,), (1,)), ((), ())), preferred_element_type=f32
         ).astype(bf)
         swap_dn[i].start()
+    ring.forward(2, 0)
 
     def own_part(i):
         part = wts[1, pl.ds(pl.multiple_of(core * HALF + i * 256, 256), 256), :]
@@ -507,34 +557,54 @@
             delta[0, rows, cols] = (d * dgelu[0, rows, cols]).astype(bf)
 
         loop(LIVE // 64, dx)
-    begin(0)
-    for ph in range(3):
-        for l in (1, 0):
-            for c in range(3):
-                ring.step_b(l, c, ph)
-        for l in (1, 0):
-            for c in range(3):
-                if ph < 2:
-                    ring.next_phase(l, c, ph)
-                else:
-                    ring.last(l, c, grads)
+    for k in (0, 1):
+        begin(ring, k, nrm_t, delta)
+    for k in (3, 0, 1):
+        ring.forward(k, 0)
+    order = (2, 3, 0, 1)
+    for k in order:
+        ring.finish(k, 0)
+    for k in order:
+        ring.forward(k, 1)
+    for k in order:
+        ring.finish(k, 1)
+    for k in order:
+        ring.last(k, grads)
     ring.wait_sends()
     scatter.wait_sends()
     for cp in (*swap_x, swap_logit, swap_stat, *swap_dn):
         cp.wait_send()
 
 
+def hand_over(grads, loss, grads_out, loss_out, grads_held, loss_held, sem):
+    into = [
+        pltpu.make_async_copy(loss, loss_held, sem.at[0]),
+        pltpu.make_async_copy(grads, grads_held, sem.at[1]),
+    ]
+    out = [
+        pltpu.make_async_copy(loss_held, loss_out, sem.at[2]),
+        pltpu.make_async_copy(grads_held, grads_out, sem.at[3]),
+    ]
+    for cp in into:
+        cp.start()
+    for a, b in zip(into, out):
+        a.wait()
+        b.start()
+    for cp in out:
+        cp.wait()
+
+
 def body(features, gains, weights, heads, lengths, owners, labels):
     slots = features.shape[0]
-    leaves, tree = flat([scratch(), scatter_scratch(), work_scratch()])
+    leaves, tree = flat([ring_scratch(), scatter_scratch(), work_scratch()])
     vmem, hbm = pl.BlockSpec(memory_space=pltpu.VMEM), pl.BlockSpec(memory_space=pl.ANY)
     grads, loss = pl.pallas_call(
         functools.partial(mega_kernel, tree),
         out_shape=(
             jax.ShapeDtypeStruct((2, 32, HALF), jnp.float32),
-            jax.ShapeDtypeStruct((1, slots), jnp.bfloat16),
+            jax.ShapeDtypeStruct((slots // 128, 128), jnp.bfloat16),
         ),
-        in_specs=[hbm, vmem, hbm, hbm, vmem, vmem, vmem],
+        in_specs=[hbm] * 7,
         out_specs=(vmem, vmem),
         scratch_shapes=leaves,
         compiler_params=pltpu.CompilerParams(
@@ -550,6 +620,15 @@
         owners,
         labels.reshape(1, slots),
     )
+    shapes = [jax.ShapeDtypeStruct(v.shape, v.dtype) for v in (grads, loss)]
+    grads, loss = pl.pallas_call(
+        hand_over,
+        out_shape=shapes,
+        in_specs=[hbm] * 2,
+        out_specs=[hbm] * 2,
+        scratch_shapes=[*[pltpu.VMEM(v.shape, v.dtype) for v in shapes], pltpu.SemaphoreType.DMA((4,))],
+        name="hand_over",
+    )(grads, loss)
     return (grads, loss.reshape(slots))
 
 

time: 119 us -> 111 us (0.933)
  Pallas kernels: 115 us -> 111 us
  local copies, waits for them, and re-layouts: 1.67 us -> 0 us
  other arithmetic: 1.25 us -> 0 us
    pallas_call x1, Pallas kernels: 115 us -> 109 us  [body(): pl.pallas_call(functools.partial(mega_kernel, tree), out_shape=(jax.Shape...]
    pallas_call x0 -> x1, Pallas kernels: none -> 1.69 us  [body(): pl.pallas_call(hand_over, out_shape=shapes, in_specs=[hbm] * 2, out_specs...]
    unnamed x1 -> x0, local copies, waits for them, and re-layouts: 1.67 us -> none
    pallas_call x1 -> x0, other arithmetic: 1.25 us -> none  [body(): pl.pallas_call(functools.partial(mega_kernel, tree), out_shape=(jax.Shape...]
where the time goes in v2:
time: 111 us
  Pallas kernels  111 us (100%)
    pallas_call x1, Pallas kernels, body(): pl.pallas_call(functools.partial(mega_kernel, tree), out_shape=(jax.Shape...  109 us

profile of v2, /device:TPU:0, one launch (start us, length us, event | category | flops | bytes accessed | tf_op | source)
XLA Modules:
  0.0 111.4 jit_solution(16554110726064215317)
XLA Ops:
  0.6 108.9 %step.1 = (f32[2,32,1024]{2,1,0:T(8,128)}, bf16[4,128]{1,0:T(4,128)(2,1)}) custom-call(bf16[512,1024]{1,0:T(8,128)(2,1)} %feats.1, f32[2,2048]{1,0:T(2,128)} %gains_hbm.1, bf16[2,2048,1024]{2,1,0:T(8,128)(2,1)} %weights.1, bf16[4,4,4,2,16,1024]{5,4,3,2,1,0:T(8,128)(2,1)} %bitcast.3, s32[1,64]{1,0:T(1,128)} %lengths_hbm.1, s32[1,64]{1,0:T(1,128)} %owners_hbm.1, ...), custom_call_target="tpu_custom_call" | custom-call | tf_op jit(solution)/shard_map/step/pallas_call | solution.py:601
  109.5 1.7 %hand_over.1 = (f32[2,32,1024]{2,1,0:T(8,128)}, bf16[4,128]{1,0:T(4,128)(2,1)}) custom-call(f32[2,32,1024]{2,1,0:T(8,128)} %get-tuple-element.6.grads, bf16[4,128]{1,0:T(4,128)(2,1)} %get-tuple-element.7.loss), custom_call_target="tpu_custom_call" | custom-call | tf_op jit(solution)/shard_map/hand_over/pallas_call | solution.py:624

commit v3 on v2

--- a/solution.py
+++ b/solution.py
@@ -14,6 +14,7 @@
 WIDTHS = ((384, 256, 384), (384, 384, 256))
 STARTS = tuple(tuple(sum(w[:k]) for k in range(3)) for w in WIDTHS)
 UNITS = (16, 4, 1)
+DIRECT = ()
 
 def blend(core, a, b):
     return a + core * (b - a)
@@ -24,10 +25,13 @@
         self.g, self.t1, self.t2, self.rx, self.tx, self.ssem, self.rsem = bufs
         self.coords = tuple((me // s) % 4 for s in STRIDES)
 
-    def dim(self, c, ph):
+    def place(self, c, ph):
         k0, k1 = (c + ph) % 3, (c + ph + 1) % 3
         stride = blend(self.core, STRIDES[k0], STRIDES[k1])
-        p = blend(self.core, self.coords[k0], self.coords[k1])
+        return blend(self.core, self.coords[k0], self.coords[k1]), stride
+
+    def dim(self, c, ph):
+        p, stride = self.place(c, ph)
         right = self.me + ((p + 1) % 4 - p) * stride
         left = self.me + ((p + 3) % 4 - p) * stride
         return p, right, left
@@ -40,10 +44,9 @@
         lo, hi = pl.ds(0, half), pl.ds(half, half)
 
         def nth(i):
-            if ph == 2:
-                src = part.at[(p + (1, 3, 2)[i]) % 4]
-                stride = blend(self.core, STRIDES[(c + 2) % 3], STRIDES[c])
-                to = (right, left, self.me + ((p + 2) % 4 - p) * stride)[i]
+            if self.direct(k, ph):
+                q = (p + (2, 1, 3)[i]) % 4
+                src, to = part.at[q], self.me + (q - p) * self.place(c, ph)[1]
             elif i < 4:
                 src = part.at[(p + (2, 1, 2, 3)[i]) % 4, (lo, hi, hi, lo)[i]]
                 to = (right, right, left, left)[i]
@@ -61,13 +64,19 @@
 
         return nth
 
+    @staticmethod
+    def direct(k, ph):
+        return ph == 2 or ph == 1 and k in DIRECT
+
     def start(self, k, c, ph):
         cp = self.copies(k, c, ph)
-        for i in (0, 1, 2) if ph == 2 else (0, 2, 1, 3):
+        for i in (0, 1, 2) if self.direct(k, ph) else (0, 2, 1, 3):
             cp(i).start()
 
     def forward(self, k, ph):
         half = UNITS[ph] // 2
+        if self.direct(k, ph):
+            return
         for c in range(3):
             n = k * 3 + c
             cp = self.copies(k, c, ph)
@@ -92,6 +101,16 @@
             cp = self.copies(k, c, ph)
             p, _, _ = self.dim(c, ph)
             part, rx, t = (self.g, self.t1)[ph][n], self.rx[ph][n], (self.t1, self.t2)[ph][n]
+            if self.direct(k, ph):
+                for i in range(3):
+                    cp(i).wait_recv()
+                for q in range(4):
+                    v = part[p, q].astype(jnp.float32)
+                    for i in range(3):
+                        v = v + rx[i, q].astype(jnp.float32)
+                    t[q, 0] = v.astype(jnp.bfloat16)
+                self.start(k, c, ph + 1)
+                continue
             for a, b, off in ((3, 4, 0), (1, 5, half)):
                 cp(a).wait_recv()
                 cp(b).wait_recv()
@@ -139,17 +158,22 @@
         for k in range(4):
             for c in range(3):
                 for ph in range(3):
-                    for i in range(3 if ph == 2 else 6):
+                    for i in range(3 if self.direct(k, ph) else 6):
                         self.copies(k, c, ph)(i).wait_send()
 
 
 def ring_scratch():
     bf = jnp.bfloat16
-    widths = [WIDTHS[k // 2][c] for k in range(4) for c in range(3)]
+    streams = [(k, WIDTHS[k // 2][c]) for k in range(4) for c in range(3)]
+
+    def arrive(k, w, ph):
+        n = UNITS[ph]
+        return (3, n, 16, w) if Ring.direct(k, ph) else (6, n // 2, 16, w)
+
     return [
-        *[[pltpu.VMEM((4, n, 16, w), bf) for w in widths] for n in UNITS],
-        [[pltpu.VMEM((6, n // 2, 16, w) if n > 1 else (3, 1, 16, w), bf) for w in widths] for n in UNITS],
-        [[pltpu.VMEM((2, n // 2, 16, w), bf) for w in widths] for n in UNITS[:2]],
+        *[[pltpu.VMEM((4, n, 16, w), bf) for _, w in streams] for n in UNITS],
+        [[pltpu.VMEM(arrive(k, w, ph), bf) for k, w in streams] for ph in range(3)],
+        [[pltpu.VMEM((2, n // 2, 16, w), bf) for _, w in streams] for n in UNITS[:2]],
         pltpu.SemaphoreType.DMA((12, 3, 6)),
         pltpu.SemaphoreType.DMA((12, 3, 6)),
     ]
@@ -186,7 +210,7 @@
 class Scatter:
     def __init__(self, ring, heads, bufs):
         self.ring, self.core, self.heads = ring, ring.core, heads
-        self.r, self.f, self.ssem, self.rsem, self.lsem = bufs
+        self.r, self.ssem, self.rsem, self.lsem = bufs
 
     def piece(self, n, ph, q, j, m):
         h, c = n // 3, n % 3
@@ -203,9 +227,6 @@
     def place(self, n, ph, j, s):
         return self.r[2][n].at[s, j] if ph == 2 else self.r[ph][n].at[j, s]
 
-    def whole(self, n, ph, k):
-        return self.r[ph][n].at[0] if k in (1, 3) else self.f[ph][n].at[0]
-
     def remote(self, n, ph, k, src, dst, to):
         return pltpu.make_async_remote_copy(
             src_ref=src,
@@ -225,21 +246,19 @@
 
     def start(self, h, ph):
         def go(m):
+            for j in range(4):
+                for c in range(3):
+                    n = h * 3 + c
+                    p, stride = self.ring.place(c, ph)
+                    for k in range(3):
+                        q = (p + (2, 1, 3)[k]) % 4
+                        self.remote(
+                            n, ph, k, self.piece(n, ph, q, j, m), self.place(n, ph, j, p),
+                            self.ring.me + (q - p) * stride,
+                        ).start()
             for c in range(3):
                 n = h * 3 + c
-                p, right, left = self.ring.dim(c, ph)
-                f = self.f[ph][n]
-                opposite = (p + 2) % 4
-                for i in range(2):
-                    self.remote(n, ph, 0, self.piece(n, ph, opposite, i, m), f.at[0, i], right).start()
-                    self.remote(n, ph, 2, self.piece(n, ph, opposite, 2 + i, m), f.at[1, i], left).start()
-                for j in range(4):
-                    self.remote(
-                        n, ph, 1, self.piece(n, ph, (p + 1) % 4, j, m), self.place(n, ph, j, p), right
-                    ).start()
-                    self.remote(
-                        n, ph, 3, self.piece(n, ph, (p + 3) % 4, j, m), self.place(n, ph, j, p), left
-                    ).start()
+                p, _ = self.ring.place(c, ph)
                 for j in range(4):
                     pltpu.make_async_copy(
                         self.piece(n, ph, p, j, m), self.place(n, ph, j, p), self.lsem.at[n, ph]
@@ -247,34 +266,22 @@
 
         self.on_core(ph, go)
 
-    def wait(self, n, ph, k, sem):
-        ref = self.whole(n, ph, k)
+    def wait(self, n, ph, sem):
+        ref = self.r[ph][n].at[0]
         pltpu.make_async_copy(ref, ref, sem).wait()
-
-    def relay(self, h, ph):
-        for c in range(3):
-            n = h * 3 + c
-            p, right, left = self.ring.dim(c, ph)
-            f = self.f[ph][n]
-            self.wait(n, ph, 0, self.rsem.at[n, ph, 0])
-            for i in range(2):
-                self.remote(n, ph, 4, f.at[0, i], self.place(n, ph, i, (p + 3) % 4), right).start()
-            self.wait(n, ph, 2, self.rsem.at[n, ph, 2])
-            for i in range(2):
-                self.remote(n, ph, 5, f.at[1, i], self.place(n, ph, 2 + i, (p + 1) % 4), left).start()
 
     def finish(self, h, ph):
         for c in range(3):
             n = h * 3 + c
-            self.wait(n, ph, 1, self.lsem.at[n, ph])
-            for k in (1, 3, 4, 5):
-                self.wait(n, ph, k, self.rsem.at[n, ph, k])
+            self.wait(n, ph, self.lsem.at[n, ph])
+            for k in range(3):
+                self.wait(n, ph, self.rsem.at[n, ph, k])
 
     def wait_sends(self):
         for n in range(6):
             for ph in range(3):
-                for k in range(6):
-                    self.wait(n, ph, k, self.ssem.at[n, ph, k])
+                for k in range(3):
+                    self.wait(n, ph, self.ssem.at[n, ph, k])
 
     def owners_of(self, c):
         return tuple(
@@ -287,9 +294,8 @@
     bf = jnp.bfloat16
     return [
         [[pltpu.VMEM((4, 4, 4, 16, WIDTHS[h][c]), bf) for h, c in hc] for _ in range(3)],
-        [[pltpu.VMEM((2, 2, 4, 16, WIDTHS[h][c]), bf) for h, c in hc] for _ in range(3)],
-        pltpu.SemaphoreType.DMA((6, 3, 6)),
-        pltpu.SemaphoreType.DMA((6, 3, 6)),
+        pltpu.SemaphoreType.DMA((6, 3, 3)),
+        pltpu.SemaphoreType.DMA((6, 3, 3)),
         pltpu.SemaphoreType.DMA((6, 3)),
     ]
 
@@ -372,10 +378,10 @@
     pl.semaphore_signal(bar, inc=1, device_id=(me, other), device_id_type=MESH)
     for s in STRIDES:
         p = (me // s) % 4
-        for step in (1, 3):
+        for step in (1, 2, 3):
             to = me + ((p + step) % 4 - p) * s
             pl.semaphore_signal(bar, inc=1, device_id=(to, core), device_id_type=MESH)
-    pl.semaphore_wait(bar, 7)
+    pl.semaphore_wait(bar, 10)
 
     swap_x = [swap(0, feats.at[pl.ds(0, LIVE)], xs[0].at[core]), swap(1, xs[1].at[core], xs[1].at[core])]
     swap_x[0].start()
@@ -443,25 +449,19 @@
     norm_layer(0)
     load[0].wait()
     main_layer(0)
-    scatter.relay(0, 0)
     turn_layer(0)
+    scatter.finish(0, 0)
+    scatter.start(0, 1)
     swap_x[1].wait_recv()
     norm_layer(1)
-    scatter.relay(1, 0)
     load[1].wait()
     main_layer(1)
-    scatter.finish(0, 0)
-    scatter.start(0, 1)
     scatter.finish(1, 0)
     scatter.start(1, 1)
     turn_layer(1)
     for h in range(2):
-        scatter.relay(h, 1)
-    for h in range(2):
         scatter.finish(h, 1)
         scatter.start(h, 2)
-    for h in range(2):
-        scatter.relay(h, 2)
 
     for h in range(2):
         scatter.finish(h, 2)

time: 111 us -> 106 us (0.955)
  Pallas kernels: 111 us -> 105 us
    pallas_call x1, Pallas kernels: 109 us -> 103 us  [body(): pl.pallas_call(functools.partial(mega_kernel, tree), out_shape=(jax.Shape...]
where the time goes in v3:
time: 106 us
  Pallas kernels  105 us (99%)
    pallas_call x1, Pallas kernels, body(): pl.pallas_call(functools.partial(mega_kernel, tree), out_shape=(jax.Shape...  103 us

profile of v3, /device:TPU:0, one launch (start us, length us, event | category | flops | bytes accessed | tf_op | source)
XLA Modules:
  0.0 105.8 jit_solution(7837425967048243385)
XLA Ops:
  0.6 103.3 %step.1 = (f32[2,32,1024]{2,1,0:T(8,128)}, bf16[4,128]{1,0:T(4,128)(2,1)}) custom-call(bf16[512,1024]{1,0:T(8,128)(2,1)} %feats.1, f32[2,2048]{1,0:T(2,128)} %gains_hbm.1, bf16[2,2048,1024]{2,1,0:T(8,128)(2,1)} %weights.1, bf16[4,4,4,2,16,1024]{5,4,3,2,1,0:T(8,128)(2,1)} %bitcast.3, s32[1,64]{1,0:T(1,128)} %lengths_hbm.1, s32[1,64]{1,0:T(1,128)} %owners_hbm.1, ...), custom_call_target="tpu_custom_call" | custom-call | tf_op jit(solution)/shard_map/step/pallas_call | solution.py:601
  104.0 1.7 %hand_over.1 = (f32[2,32,1024]{2,1,0:T(8,128)}, bf16[4,128]{1,0:T(4,128)(2,1)}) custom-call(f32[2,32,1024]{2,1,0:T(8,128)} %get-tuple-element.6.grads, bf16[4,128]{1,0:T(4,128)(2,1)} %get-tuple-element.7.loss), custom_call_target="tpu_custom_call" | custom-call | tf_op jit(solution)/shard_map/hand_over/pallas_call | solution.py:624

commit v4 on v3

--- a/solution.py
+++ b/solution.py
@@ -154,12 +154,11 @@
 
             lax.fori_loop(0, count // n, go, 0)
 
-    def wait_sends(self):
+    def wait_sends(self, ph):
         for k in range(4):
             for c in range(3):
-                for ph in range(3):
-                    for i in range(3 if self.direct(k, ph) else 6):
-                        self.copies(k, c, ph)(i).wait_send()
+                for i in range(3 if self.direct(k, ph) else 6):
+                    self.copies(k, c, ph)(i).wait_send()
 
 
 def ring_scratch():
@@ -321,8 +320,8 @@
         pltpu.VMEM((LIVE, HALF), f32),
         pltpu.VMEM((2, LIVE, HALF), bf),
         pltpu.VMEM((2, 32, LIVE), f32),
-        pltpu.VMEM((LIVE, 128), f32),
-        pltpu.VMEM((LIVE, HALF), bf),
+        pltpu.VMEM((LIVE, 128), bf),
+        pltpu.VMEM((6, LIVE, HALF), bf),
         pltpu.VMEM((2, LIVE, 128), f32),
         pltpu.VMEM((2, 4, LIVE, 256), bf),
         pltpu.VMEM((4, LIVE, 256), f32),
@@ -402,7 +401,7 @@
     here = (slot < ends) & (slot >= ends - lens_down)
     slot_owner = jnp.sum(jnp.where(here, down(owners[...]), 0), 0, keepdims=True)
     slot_len = jnp.sum(jnp.where(here, lens_down, 0), 0, keepdims=True)
-    owner_down[...] = jnp.broadcast_to(slot_owner.astype(f32), (128, LIVE)).T
+    owner_down[...] = jnp.broadcast_to(slot_owner.astype(f32), (128, LIVE)).T.astype(bf)
 
     def norm_layer(l):
         def norm(i):
@@ -496,17 +495,17 @@
 
     group = lax.broadcasted_iota(jnp.int32, (1, 128), 1) // 16
     for h in range(2):
-        tiled = jnp.concatenate([dlogits[16 * h : 16 * h + 16]] * 8, axis=0).T
+        tiled = jnp.concatenate([dlogits[16 * h : 16 * h + 16]] * 8, axis=0).T.astype(bf)
         for c in range(3):
             w0, w = STARTS[h][c], WIDTHS[h][c]
             sa, sb, sc = scatter.owners_of(c)
             for j in range(8):
                 owner = (group % 4) * sa + (2 * (j % 2) + group // 4) * sb + (j // 2) * sc
-                spread[:, 128 * j : 128 * j + 128] = jnp.where(
-                    owner_down[...] == owner.astype(f32), tiled, 0.0
-                ).astype(bf)
+                spread[3 * h + c, :, 128 * j : 128 * j + 128] = jnp.where(
+                    owner_down[...] == owner.astype(f32).astype(bf), tiled, jnp.zeros((), bf)
+                )
             block = scatter.r[2][h * 3 + c]
-            grad = jnp.dot(spread[...], block[...].reshape(1024, w), preferred_element_type=f32)
+            grad = jnp.dot(spread[3 * h + c], block[...].reshape(1024, w), preferred_element_type=f32)
             cols = slice(w0, w0 + w)
             up[:, cols] = grad if h == 0 else up[:, cols] + grad
 
@@ -559,21 +558,24 @@
         loop(LIVE // 64, dx)
     for k in (0, 1):
         begin(ring, k, nrm_t, delta)
-    for k in (3, 0, 1):
+    for k in (3, 0):
         ring.forward(k, 0)
+    scatter.wait_sends()
+    for cp in (*swap_x, swap_logit, swap_stat, *swap_dn):
+        cp.wait_send()
+    ring.forward(1, 0)
     order = (2, 3, 0, 1)
     for k in order:
         ring.finish(k, 0)
     for k in order:
         ring.forward(k, 1)
+    ring.wait_sends(0)
     for k in order:
         ring.finish(k, 1)
+    ring.wait_sends(1)
     for k in order:
         ring.last(k, grads)
-    ring.wait_sends()
-    scatter.wait_sends()
-    for cp in (*swap_x, swap_logit, swap_stat, *swap_dn):
-        cp.wait_send()
+    ring.wait_sends(2)
 
 
 def hand_over(grads, loss, grads_out, loss_out, grads_held, loss_held, sem):

time: 106 us -> 105 us (level)
  no operation moved by 1% of the time
where the time goes in v4:
time: 105 us
  Pallas kernels  104 us (99%)
    pallas_call x1, Pallas kernels, body(): pl.pallas_call(functools.partial(mega_kernel, tree), out_shape=(jax.Shape...  103 us

profile of v4, /device:TPU:0, one launch (start us, length us, event | category | flops | bytes accessed | tf_op | source)
XLA Modules:
  0.0 105.0 jit_solution(9186350675989439268)
XLA Ops:
  0.6 102.7 %step.1 = (f32[2,32,1024]{2,1,0:T(8,128)}, bf16[4,128]{1,0:T(4,128)(2,1)}) custom-call(bf16[512,1024]{1,0:T(8,128)(2,1)} %feats.1, f32[2,2048]{1,0:T(2,128)} %gains_hbm.1, bf16[2,2048,1024]{2,1,0:T(8,128)(2,1)} %weights.1, bf16[4,4,4,2,16,1024]{5,4,3,2,1,0:T(8,128)(2,1)} %bitcast.3, s32[1,64]{1,0:T(1,128)} %lengths_hbm.1, s32[1,64]{1,0:T(1,128)} %owners_hbm.1, ...), custom_call_target="tpu_custom_call" | custom-call | tf_op jit(solution)/shard_map/step/pallas_call | solution.py:603
  103.3 1.7 %hand_over.1 = (f32[2,32,1024]{2,1,0:T(8,128)}, bf16[4,128]{1,0:T(4,128)(2,1)}) custom-call(f32[2,32,1024]{2,1,0:T(8,128)} %get-tuple-element.6.grads, bf16[4,128]{1,0:T(4,128)(2,1)} %get-tuple-element.7.loss), custom_call_target="tpu_custom_call" | custom-call | tf_op jit(solution)/shard_map/hand_over/pallas_call | solution.py:626
